TPU v7x, 256 devices: a whole 4x4x8 slice. The times are simulated.
256 devices in a mesh: dp: 2 (over core), context: 32 (over y, z), tensor: 4 (over x).
Axes of the slice: x: 4, y: 4, z: 8, core: 2. Of those that a mesh axis runs over, the one named last changes fastest.
Arguments:
- mixer_input: bfloat16 [16384, 5120], P(('dp', 'context'), 'tensor'), parts along dimension 0, may hold values from -6 to 6
- gate_z: bfloat16 [16384, 4096], P(('dp', 'context'), 'tensor'), parts along dimension 0, may hold values from -6 to 6
- dt_raw: float32 [16384, 64], P(('dp', 'context'), 'tensor'), parts along dimension 0, may hold values from -6 to 6
- dt_bias: float32 [64], P('tensor'), may hold values from -3 to 3
- a_log: float32 [64], P('tensor'), may hold values from -11 to -2.5
- d_skip: float32 [64], P('tensor'), may hold values from 0.5 to 1.5
- conv_weight: float32 [4, 5120], P(None, 'tensor'), may hold values from -3 to 3
- conv_bias: float32 [5120], P('tensor'), may hold values from -2 to 2
- norm_gain: float32 [4096], P('tensor'), may hold values from 0.25 to 1.75
- w_out: bfloat16 [4096, 4096], P('tensor'), may hold values from -0.09375 to 0.09375
- residual: bfloat16 [16384, 4096], P(('dp', 'context'), 'tensor'), parts along dimension 0, may hold values from -6 to 6
- attn_gain: float32 [4096], replicated, may hold values from 0.1 to 1.9
- w_query: bfloat16 [4096, 2048], P('context', 'tensor'), may hold values from -4 to 4
- w_key: bfloat16 [4096, 512], P('context', 'tensor'), may hold values from -4 to 4
- value_weight: bfloat16 [4096, 512], P('context', 'tensor'), may hold values from -0.09375 to 0.09375
- doc_ids: int32 [16384], P(('dp', 'context')), parts along dimension 0, may hold values from 0 to 15, never falling along the last dimension, each value on 1 to 4352 neighbouring positions
- owners: int32 [64, 32], P(('dp', 'context')), parts along dimension 0, may hold values from 0 to 31, each once within a row
Outputs:
- hidden_out: bfloat16 [16384, 4096], P(('dp', 'context'), 'tensor'), parts along dimension 0
- attended: bfloat16 [16384, 2048], P(('dp', 'context'), 'tensor'), parts along dimension 0
There are 2 independent parts, one for each index of `dp`. A program takes and returns all parts, laid end to end along the dimension named above; an argument that names none is the same for every part. Nothing has to cross between parts.
Inputs may be any that keep to these rules, and one draw needn't show every extreme that they name: `doc_ids`: ids never fall along the sequence; each document has 1 to 4352 tokens and one has exactly 4352. `owners`: row i names, for each of the 32 blocks of 8 tokens of context index i, the context index that owns it; each row is a permutation.
All inputs are finite; a program needn't handle non-finite values.
Results may differ from a plain program's by a relative error of at most 0.04.
The roundings to bfloat16 on the way count: a program that leaves them out, or rounds other values in their place, can miss the bound.
Values may be sent and summed in bfloat16 or wider, within the bound.
A program may use at most 128 MiB of HBM per device.

v0:
```python
import math

import jax
import jax.numpy as jnp
from jax import lax
from jax.sharding import PartitionSpec as P

P_SIZE = 64
NS = 128
HEAD_DIMENSION = 128


epsilon = 1e-05
rope_base = 500000.0


def shifted(value, axis, steps):
    count = lax.axis_size(axis)
    initial, last = (max(0, -steps), min(count, count - steps))
    return lax.ppermute(value, axis, [(source, source + steps) for source in range(initial, last)])


def carried_in(part, axis, combine, identity):
    place = lax.axis_index(axis)
    gathered = jax.tree.map(lambda a: lax.all_gather(a, axis), part)
    state = jax.tree.map(lambda a, e: jnp.zeros_like(a) + jnp.asarray(e, a.dtype), part, identity)

    def one(turn, state):
        return combine(
            state, jax.tree.map(lambda a: lax.dynamic_index_in_dim(a, turn, 0, False), gathered)
        )

    return lax.fori_loop(0, place, one, state)


def rotate(value_matrix, positions):
    heads = value_matrix.shape[1] // HEAD_DIMENSION
    shaped = value_matrix.reshape(value_matrix.shape[0], heads, HEAD_DIMENSION)
    half_width = HEAD_DIMENSION // 2
    freqs = jnp.exp(
        jnp.arange(half_width, dtype=jnp.float32) * (-2.0 * math.log(rope_base) / HEAD_DIMENSION)
    )
    angles = positions.astype(jnp.float32)[:, None] * freqs[None, :]
    cosine = jnp.cos(angles)[:, None, :]
    sine = jnp.sin(angles)[:, None, :]
    first_half = shaped[:, :, :half_width]
    second_half = shaped[:, :, half_width:]
    rotated = jnp.concatenate(
        [first_half * cosine - second_half * sine, second_half * cosine + first_half * sine],
        axis=-1,
    )
    return rotated.reshape(value_matrix.shape)


def chain(earlier, later):
    return (earlier[0] * later[0], later[0][:, None, None] * earlier[1] + later[1])


def per_device(
    mixer_input,
    gate_z,
    dt_raw,
    dt_bias,
    a_log,
    d_skip,
    conv_weight,
    conv_bias,
    norm_gain,
    w_out,
    residual,
    attn_gain,
    w_query,
    w_key,
    value_weight,
    doc_ids,
    owners,
):
    row_count = mixer_input.shape[0]
    devices = lax.axis_size("context")
    position_here = lax.axis_index("context")
    first_row = position_here * row_count
    all_docs = lax.all_gather(doc_ids, "context", axis=0, tiled=True)
    lag = conv_weight.shape[0] - 1
    before_rows = shifted(mixer_input[row_count - lag :], "context", 1)
    before_docs = jnp.where(
        position_here > 0,
        lax.dynamic_slice_in_dim(all_docs, jnp.maximum(first_row - lag, 0), lag),
        -1,
    )
    prev_doc = before_docs[lag - 1]
    extended = jnp.concatenate([before_rows, mixer_input]).astype(jnp.float32)
    extended_docs = jnp.concatenate([before_docs, doc_ids])
    running = jnp.broadcast_to(conv_bias, mixer_input.shape)
    for offset in range(lag + 1):
        same_doc = extended_docs[offset : offset + row_count] == doc_ids
        running = running + conv_weight[offset] * jnp.where(
            same_doc[:, None], extended[offset : offset + row_count], 0.0
        )
    conv_out = jax.nn.silu(running).astype(jnp.bfloat16)
    heads = dt_raw.shape[1]
    width_x = heads * P_SIZE
    inputs_x = conv_out[:, :width_x].reshape(row_count, heads, P_SIZE)
    in_b = conv_out[:, width_x : width_x + NS]
    out_c = conv_out[:, width_x + NS :]
    step_size = jax.nn.softplus(dt_raw + dt_bias)
    cumul = jnp.cumsum(-step_size * jnp.exp(a_log), axis=0)
    intersection = lax.dot_general(
        out_c, in_b, (((1,), (1,)), ((), ())), preferred_element_type=jnp.float32
    )
    row_ids = jnp.arange(row_count, dtype=jnp.int32)
    allowed = (doc_ids[:, None] == doc_ids[None, :]) & (row_ids[:, None] >= row_ids[None, :])
    decays = jnp.exp(jnp.where(allowed[None], cumul.T[:, :, None] - cumul.T[:, None, :], -jnp.inf))
    weights = decays * intersection[None] * step_size.T[:, None, :]
    inputs_float = inputs_x.astype(jnp.float32)
    outputs = jnp.einsum("hts,shp->thp", weights, inputs_float, precision=lax.Precision.HIGHEST)
    end_weight = (
        jnp.exp(cumul[-1][None, :] - cumul)
        * (doc_ids == doc_ids[-1]).astype(jnp.float32)[:, None]
        * step_size
    )
    state = jnp.einsum(
        "sh,shp,sn->hpn",
        end_weight,
        inputs_float,
        in_b.astype(jnp.float32),
        precision=lax.Precision.HIGHEST,
    )
    through = jnp.exp(cumul[-1]) * (doc_ids[-1] == prev_doc).astype(jnp.float32)
    through_in, incoming = carried_in(
        (through, state), "context", chain, (jnp.ones_like(through), jnp.zeros_like(state))
    )
    carry_on = (doc_ids == prev_doc).astype(jnp.float32)
    outputs = outputs + jnp.exp(cumul)[:, :, None] * carry_on[:, None, None] * jnp.einsum(
        "tn,hpn->thp", out_c.astype(jnp.float32), incoming, precision=lax.Precision.HIGHEST
    )
    outputs = outputs + d_skip[None, :, None] * inputs_float
    gated = outputs.reshape(row_count, width_x) * jax.nn.silu(gate_z.astype(jnp.float32))
    power = jnp.mean(gated * gated, axis=-1, keepdims=True)
    normed_ssm = (gated * lax.rsqrt(power + epsilon) * norm_gain).astype(jnp.bfloat16)
    partial_value = jnp.dot(normed_ssm, w_out, preferred_element_type=jnp.float32)
    model_width = partial_value.shape[1]
    share_width = residual.shape[1]
    column = lax.axis_index("tensor") * share_width
    share = lax.psum_scatter(partial_value, "tensor", scatter_dimension=1, tiled=True)
    hidden_out = (residual.astype(jnp.float32) + share).astype(jnp.bfloat16)
    stream_float = hidden_out.astype(jnp.float32)
    squares = lax.psum(jnp.sum(stream_float * stream_float, axis=-1), "tensor")
    gain_here = lax.dynamic_slice_in_dim(attn_gain, column, share_width)
    normed_share = (
        stream_float * lax.rsqrt(squares / model_width + epsilon)[:, None] * gain_here
    ).astype(jnp.bfloat16)
    normed = lax.all_gather(normed_share, "tensor", axis=1, tiled=True)
    pieces = (
        lax.all_gather(w_query, "context", axis=0, tiled=True),
        lax.all_gather(w_key, "context", axis=0, tiled=True),
        lax.all_gather(value_weight, "context", axis=0, tiled=True),
    )
    query_raw, key_raw, value_raw = tuple(
        (
            jnp.dot(normed, weight_piece, preferred_element_type=jnp.float32)
            for weight_piece in pieces
        )
    )
    positions = first_row + jnp.arange(row_count, dtype=jnp.int32)
    queries = rotate(query_raw, positions).astype(jnp.bfloat16)
    key_matrix = rotate(key_raw, positions).astype(jnp.bfloat16)
    value_matrix = value_raw.astype(jnp.bfloat16)
    scaling = HEAD_DIMENSION ** (-0.5)
    out_width = queries.shape[1]
    block_rows = row_count // devices
    device_ids = jnp.arange(devices, dtype=jnp.int32)
    own_list = owners[0]
    chosen = jnp.sum(
        jnp.where(own_list[None, :] == device_ids[:, None], device_ids[None, :], 0), axis=1
    )
    number = queries.shape[0]
    kv_heads = key_matrix.shape[1] // HEAD_DIMENSION
    group_size = queries.shape[1] // HEAD_DIMENSION // kv_heads
    shaped_query = queries.reshape(number, kv_heads, group_size, HEAD_DIMENSION)
    pos_top = jnp.max(positions)
    doc_low = jnp.min(doc_ids)
    doc_high = jnp.max(doc_ids)
    initial = (
        jnp.full((kv_heads, group_size, number), -1e30, jnp.float32),
        jnp.zeros((kv_heads, group_size, number), jnp.float32),
        jnp.zeros((kv_heads, group_size, number, HEAD_DIMENSION), jnp.float32),
    )
    key_piece = lax.all_gather(key_matrix, "context", axis=0, tiled=True)
    value_piece = lax.all_gather(value_matrix, "context", axis=0, tiled=True)
    span = key_piece.shape[0]
    key_pos = jnp.arange(span, dtype=jnp.int32)

    def update(state_tuple):
        best, denom, accum = state_tuple
        scores = (
            jnp.einsum(
                "qkgd,rkd->kgqr",
                shaped_query,
                key_piece.reshape(span, kv_heads, HEAD_DIMENSION),
                preferred_element_type=jnp.float32,
            )
            * scaling
        )
        usable = (doc_ids[:, None] == all_docs[None, :]) & (key_pos[None, :] <= positions[:, None])
        fresh = jnp.maximum(best, jnp.max(jnp.where(usable, scores, -1e30), axis=-1))
        probs = jnp.where(usable, jnp.exp(scores - fresh[..., None]), 0.0)
        denom = jnp.sum(probs, axis=-1)
        accum = jnp.einsum(
            "kgqr,rkd->kgqd",
            probs.astype(jnp.bfloat16),
            value_piece.reshape(span, kv_heads, HEAD_DIMENSION),
            preferred_element_type=jnp.float32,
        )
        return (fresh, denom, accum)

    skipping = (jnp.int32(0) > pos_top) | (all_docs[span - 1] < doc_low) | (all_docs[0] > doc_high)
    best, denom, accum = lax.cond(skipping, lambda state_tuple: state_tuple, update, initial)
    local_out = (
        (accum / denom[..., None]).transpose(2, 0, 1, 3).reshape(number, -1).astype(jnp.bfloat16)
    )
    outgoing = jnp.take(local_out.reshape(devices, block_rows, out_width), chosen, axis=0)
    attended = lax.all_to_all(outgoing, "context", split_axis=0, concat_axis=0, tiled=True).reshape(
        row_count, out_width
    )
    return (hidden_out, attended)


def solution(mesh):
    in_specs = (
        P(("dp", "context"), "tensor"),
        P(("dp", "context"), "tensor"),
        P(("dp", "context"), "tensor"),
        P("tensor"),
        P("tensor"),
        P("tensor"),
        P(None, "tensor"),
        P("tensor"),
        P("tensor"),
        P("tensor", None),
        P(("dp", "context"), "tensor"),
        P(),
        P("context", "tensor"),
        P("context", "tensor"),
        P("context", "tensor"),
        P(("dp", "context")),
        P(("dp", "context"), None),
    )
    out_specs = (P(("dp", "context"), "tensor"), P(("dp", "context"), "tensor"))
    return jax.shard_map(
        per_device, mesh=mesh, in_specs=in_specs, out_specs=out_specs, check_vma=False
    )
```

profile of v0, /device:TPU:32, one launch (start us, length us, event | category | flops | bytes accessed | tf_op | source)
XLA Modules:
  0.0 803.7 jit_solution(12720084516224285079)
XLA Ops:
  7.2 0.7 slice.82
  8.0 3.8 collective-permute-start
  11.8 44.5 %all-gather.2 = s32[32,1,256]{2,1,0:T(1,128)S(1)} all-gather(s32[1,1,256]{2,1,0:T(1,128)} %bitcast.122), channel_id=1, replica_groups=mesh['dp'=2,'context'=32,'tensor'=4] {'context'}, dimensions={0}, use_global_device_ids=true | all-gather | bytes 33792 | tf_op jit(solution)/shard_map/all_gather | solution.py:82
  56.4 0.6 slice.97
  57.0 0.8 pad_add_fusion
  57.7 1.3 slice.99
  60.4 2.1 compare_convert_fusion.1
  62.5 0.7 exp.43
  63.1 0.8 copy_bitcast_fusion.1
  64.0 0.6 reduce-window.6
  65.0 0.8 multiply_multiply_fusion
  65.8 0.9 slice_reduce_fusion.5
  66.8 1.2 maximum_convert_fusion
  68.0 1.1 multiply_convert_fusion
  69.4 1.5 fusion.44
  71.0 36.9 %all-gather.3 = f32[32,1,16]{2,1,0:T(1,128)S(1)} all-gather(f32[1,1,16]{2,1,0:T(1,128)S(1)} %bitcast.126), channel_id=1, replica_groups=mesh['dp'=2,'context'=32,'tensor'=4] {'context'}, dimensions={0}, use_global_device_ids=true | all-gather | bytes 2112 | tf_op jit(solution)/shard_map/all_gather | solution.py:25
  108.2 4.2 fusion.32
  112.5 95.6 %all-gather.22.cloned.1.call-done = f32[512,64,128]{2,1,0:T(8,128)} async-done(((f32[16,64,128]{2,1,0:T(8,128)}), f32[512,64,128]{2,1,0:T(8,128)}) %all-gather.22.cloned.1.call-update) | async-done | bytes 16777232 | tf_op jit(solution)/shard_map/all_gather | solution.py:25
  208.1 1.2 while.12
  208.1 1.2 bitcast_add_fusion.2
  209.4 1.9 fusion.36
  212.0 7.9 fusion.52
  220.0 0.7 all-gather.16.cloned.1.call-update
  220.8 82.3 %reduce-scatter.2.cloned.1.call-done = f32[256,1024]{1,0:T(8,128)} async-done(((f32[256,4096]{1,0:T(8,128)}), f32[256,1024]{1,0:T(8,128)}) %reduce-scatter.2.cloned.1.call-update) | async-done | bytes 1048592 | tf_op jit(solution)/shard_map/reduce_scatter | solution.py:144
  303.1 1.5 fusion.49
  304.6 8.6 %psum.7 = f32[256]{0:T(256)S(1)} all-reduce(f32[256]{0:T(256)S(1)} %get-tuple-element.120), channel_id=1, replica_groups=mesh['dp'=2,'context'=32,'tensor'=4] {'tensor'}, use_global_device_ids=true, to_apply=%region_11.12 | all-reduce | flops 256 | bytes 2048 | tf_op jit(solution)/shard_map/psum | solution.py:147
  313.2 1.0 fusion.51
  315.5 65.5 %all-gather.16.cloned.1.call-done = bf16[4096,128]{1,0:T(8,128)(2,1)} async-done(((bf16[128,128]{1,0:T(8,128)(2,1)}), bf16[4096,128]{1,0:T(8,128)(2,1)}) %all-gather.16.cloned.1.call-update) | async-done | bytes 1048592 | tf_op jit(solution)/shard_map/all_gather | solution.py:155
  380.9 33.4 %all-gather.12.cloned.1.call-done = bf16[256,4096]{1,0:T(8,128)(2,1)} async-done(((bf16[256,1024]{1,0:T(8,128)(2,1)}), bf16[256,4096]{1,0:T(8,128)(2,1)}) %all-gather.12.cloned.1.call-update) | async-done | bytes 2097168 | tf_op jit(solution)/shard_map/all_gather | solution.py:152
  414.3 2.8 convolution_bitcast_fusion
  417.5 0.6 pad_maximum_fusion.1
  418.4 73.9 %all-gather.18.cloned.1.call-done = bf16[4096,128]{1,0:T(8,128)(2,1)} async-done(((bf16[128,128]{1,0:T(8,128)(2,1)}), bf16[4096,128]{1,0:T(8,128)(2,1)}) %all-gather.18.cloned.1.call-update) | async-done | bytes 1048592 | tf_op jit(solution)/shard_map/all_gather | solution.py:156
  492.3 2.6 convolution_convert_fusion
  494.9 0.6 fusion.74
  496.1 0.7 fusion.80
  496.8 0.6 fusion.82
  500.5 74.2 %all-gather.14.cloned.1.call-done = bf16[4096,512]{1,0:T(8,128)(2,1)} async-done(((bf16[128,512]{1,0:T(8,128)(2,1)}), bf16[4096,512]{1,0:T(8,128)(2,1)}) %all-gather.14.cloned.1.call-update) | async-done | bytes 4194320 | tf_op jit(solution)/shard_map/all_gather | solution.py:154
  574.7 3.4 fusion.83
  579.0 70.3 %all-gather.24.cloned.1.call-done = bf16[8192,1,128]{0,2,1:T(8,128)(2,1)} async-done(((bf16[256,1,128]{0,2,1:T(8,128)(2,1)}), bf16[8192,1,128]{0,2,1:T(8,128)(2,1)}) %all-gather.24.cloned.1.call-update) | async-done | bytes 2097168 | tf_op jit(solution)/shard_map/all_gather | solution.py:188
  649.3 79.1 %all-gather.20.cloned.1.call-done = bf16[8192,128]{1,0:T(8,128)(2,1)} async-done(((bf16[256,128]{1,0:T(8,128)(2,1)}), bf16[8192,128]{1,0:T(8,128)(2,1)}) %all-gather.20.cloned.1.call-update) | async-done | bytes 2097168 | tf_op jit(solution)/shard_map/all_gather | solution.py:189
  728.3 49.0 %conditional.1 = (f32[1,4,256]{2,1,0:T(4,128)S(1)}, f32[1,4,256,128]{3,2,1,0:T(8,128)S(1)}) conditional(s32[]{:T(128)} %convert_element_type.82, (s32[256]{0:T(256)S(1)}, s32[8192]{0:T(1024)S(1)}, s32[8192]{0:T(1024)S(1)}, s32[256]{0:T(256)S(1)}, bf16[256,4,128]{2,0,1:T(8,128)(2,1)S(1)}, /*index=5*/bf16[8192,128]{0,1:T(8,128)(2,1)}, ...), branch_computations={%region_12.15_spmd, %region_15.16_spmd} | conditional | flops 4393532416 | bytes 122513456 | solution.py:217
  728.3 5.6 compare_and_fusion
  733.9 13.7 %fusion = (f32[4,256]{1,0:T(4,128)S(1)}, f32[8192,256,4]{1,0,2:T(8,128)}) fusion(pred[256,8192]{0,1:T(8,128)(4,1)S(1)} %compare_and_fusion, bf16[256,4,128]{2,0,1:T(8,128)(2,1)S(1)} %get-tuple-element.64, bf16[8192,128]{0,1:T(8,128)(2,1)S(1)} %copy-done.7), kind=kOutput, calls=%fused_computation.5 | convolution fusion | flops 2172648448 | bytes 38014976 | tf_op jit(solution)/shard_map/cond/branch_0_fun/qkgd,rkd->kgqr/dot_general | solution.py:196
  747.6 15.2 %fusion.12 = f32[1,4,256,128]{3,2,1,0:T(8,128)S(1)} fusion(bf16[8192,128]{1,0:T(8,128)(2,1)} %get-tuple-element.65, f32[8192,256,4]{1,0,2:T(8,128)} %get-tuple-element.123, f32[4,256]{1,0:T(4,128)S(1)} %broadcast_maximum_fusion, pred[256,8192]{0,1:T(8,128)(4,1)S(1)} %compare_and_fusion), kind=kOutput, calls=%fused_computation.17 | convolution fusion | flops 2181038080 | bytes 38277120 | tf_op jit(solution)/shard_map/cond/branch_0_fun/kgqr,rkd->kgqd/dot_general | solution.py:208
  762.8 14.5 %fusion.4 = f32[4,256]{1,0:T(4,128)S(1)} fusion(f32[8192,256,4]{1,0,2:T(8,128)} %get-tuple-element.123, f32[4,256]{1,0:T(4,128)S(1)} %broadcast_maximum_fusion, pred[256,8192]{0,1:T(8,128)(4,1)S(1)} %compare_and_fusion), kind=kLoop, calls=%fused_computation.9 | loop fusion | flops 33553408 | bytes 35659776 | tf_op jit(solution)/shard_map/cond/branch_0_fun/reduce_sum | solution.py:207
  777.9 0.6 gather_fusion
  778.6 17.6 %all_to_all.5 = bf16[32,8,512]{2,1,0:T(8,128)(2,1)S(1)} all-to-all(bf16[32,8,512]{2,1,0:T(8,128)(2,1)S(1)} %broadcast_select_fusion), channel_id=1, replica_groups=mesh['dp'=2,'context'=32,'tensor'=4] {'context'}, dimensions={0} | all-to-all | bytes 524288 | tf_op jit(solution)/shard_map/all_to_all | solution.py:222
  796.1 0.7 copy.83
  (73 shorter events, 6.0 us)
Async XLA Ops:
  7.2 60.9 %copy-start.5 = (f32[1280]{0:T(1024)S(1)}, f32[1280]{0:T(1024)}, u32[]{:S(2)}) copy-start(f32[1280]{0:T(1024)} %param.28) | copy-start | bytes 15364
  7.2 200.9 %all-gather.22.cloned.1.call-start = ((), (), s32[]{:S(2)}) async-start(), calls=%async_computation.8 | async-start | bytes 17301504 | tf_op jit(solution)/shard_map/all_gather | solution.py:25
  8.0 58.8 %collective-permute-start = (bf16[3,1280]{1,0:T(4,128)(2,1)S(1)}, bf16[3,1280]{1,0:T(4,128)(2,1)S(1)}, u32[]{:S(2)}, u32[]{:S(2)}) collective-permute-start(bf16[3,1280]{1,0:T(4,128)(2,1)S(1)} %slice.82), channel_id=1, source_target_pairs={{0,4},{4,8},{8,12},{12,16},{16,20},{20,24},{24,28},{28,32},{32,36}... | collective-permute-start | bytes 23048 | tf_op jit(solution)/shard_map/ppermute | solution.py:20
  69.2 38.8 %copy-start.4 = (s32[256]{0:T(256)S(1)}, s32[256]{0:T(256)}, u32[]{:S(2)}) copy-start(s32[256]{0:T(256)} %param.36) | copy-start | bytes 3076
  70.9 232.2 %reduce-scatter.2.cloned.1.call-start = ((), (), s32[]{:S(2)}) async-start(), calls=%async_computation.2 | async-start | bytes 5242880 | tf_op jit(solution)/shard_map/reduce_scatter | solution.py:144
  208.1 1.3 copy-start.6
  209.4 2.2 copy-start.2
  211.2 0.8 copy-start.8
  219.9 83.2 %copy-start.3 = (bf16[256,1024]{1,0:T(8,128)(2,1)S(1)}, bf16[256,1024]{1,0:T(8,128)(2,1)}, u32[]{:S(2)}) copy-start(bf16[256,1024]{1,0:T(8,128)(2,1)} %param.31) | copy-start | bytes 1572868
  220.0 161.0 %all-gather.16.cloned.1.call-start = ((), (), s32[]{:S(2)}) async-start(), calls=%async_computation.5 | async-start | bytes 1081344 | tf_op jit(solution)/shard_map/all_gather | solution.py:155
  220.7 193.6 %all-gather.12.cloned.1.call-start = ((), (), s32[]{:S(2)}) async-start(), calls=%async_computation.3 | async-start | bytes 2621440 | tf_op jit(solution)/shard_map/all_gather | solution.py:152
  220.7 92.4 %dynamic-slice-start = ((f32[4096]{0:T(1024)}, s32[]{:T(128)}), f32[1024]{0:T(1024)S(1)}, s32[]{:S(2)}) async-start(f32[4096]{0:T(1024)} %param.32, s32[]{:T(128)} %select_n.78), calls=%async_computation.10 | async-start | bytes 8704 | tf_op jit(solution)/shard_map/dynamic_slice | solution.py:148
  304.6 112.6 %copy-start.1 = (bf16[256,1024]{1,0:T(8,128)(2,1)}, bf16[256,1024]{1,0:T(8,128)(2,1)S(1)}, u32[]{:S(2)}) copy-start(bf16[256,1024]{1,0:T(8,128)(2,1)S(1)} %get-tuple-element.209) | copy-start | bytes 1572868
  314.2 178.1 %all-gather.18.cloned.1.call-start = ((), (), s32[]{:S(2)}) async-start(), calls=%async_computation.6 | async-start | bytes 1081344 | tf_op jit(solution)/shard_map/all_gather | solution.py:156
  314.8 259.9 %all-gather.14.cloned.1.call-start = ((), (), s32[]{:S(2)}) async-start(), calls=%async_computation.4 | async-start | bytes 4325376 | tf_op jit(solution)/shard_map/all_gather | solution.py:154
  315.4 333.9 %all-gather.24.cloned.1.call-start = ((), (), s32[]{:S(2)}) async-start(), calls=%async_computation.9 | async-start | bytes 2162688 | tf_op jit(solution)/shard_map/all_gather | solution.py:188
  414.3 78.0 %copy-start = (bf16[256,4096]{1,0:T(8,128)(2,1)S(1)}, bf16[256,4096]{1,0:T(8,128)(2,1)}, u32[]{:S(2)}) copy-start(bf16[256,4096]{1,0:T(8,128)(2,1)} %all-gather.12.cloned.1.call-done) | copy-start | bytes 6291460
  417.2 82.7 %copy-start.9 = (s32[1,32]{1,0:T(1,128)S(1)}, s32[1,32]{1,0:T(1,128)}, u32[]{:S(2)}) copy-start(s32[1,32]{1,0:T(1,128)} %param.37) | copy-start | bytes 388
  418.2 310.1 %all-gather.20.cloned.1.call-start = ((), (), s32[]{:S(2)}) async-start(), calls=%async_computation.7 | async-start | bytes 2162688 | tf_op jit(solution)/shard_map/all_gather | solution.py:189
  728.3 5.6 copy-start.7
Sparse Core Ops, SparseCore 0:
  71.0 136.9 all-gather.21
  220.1 82.9 reduce-scatter.1
  305.7 75.2 all-gather.15
  382.6 31.6 all-gather.11
  416.8 75.4 all-gather.17
  494.8 79.8 all-gather.13
  577.7 71.4 all-gather.23
  651.8 76.4 all-gather.19
where the time goes:
time: 806 us; the launch traced here: 804 us
  waiting for transfers between devices  576 us (71%)
  blocking collectives  108 us (13%)
  matrix products  53.3 us (7%)
  other arithmetic  35.6 us (4%)
  between operations  18.9 us (2%)
    all_gather x1, waiting for transfers between devices, carried_in(): gathered = jax.tree.map(lambda a: lax.all_gather(a, axis), part)  95.6 us
    reduce_scatter x1, waiting for transfers between devices, per_device(): lax.psum_scatter(partial_value, 'tensor', scatter_dimension=1, tiled=True)  82.3 us
    all_gather x1, waiting for transfers between devices, per_device(): value_piece = lax.all_gather(value_matrix, 'context', axis=0, tiled=True)  79.1 us
    all_gather x1, waiting for transfers between devices, per_device(): lax.all_gather(w_query, 'context', axis=0, tiled=True)  74.2 us
    all_gather x1, waiting for transfers between devices, per_device(): lax.all_gather(value_weight, 'context', axis=0, tiled=True)  73.9 us
    all_gather x1, waiting for transfers between devices, per_device(): key_piece = lax.all_gather(key_matrix, 'context', axis=0, tiled=True)  70.3 us
    all_gather x1, waiting for transfers between devices, per_device(): lax.all_gather(w_key, 'context', axis=0, tiled=True)  65.5 us
    all_gather x1, blocking collectives, per_device(): all_docs = lax.all_gather(doc_ids, 'context', axis=0, tiled=True)  44.5 us
  transfers between devices with their start and end apart: 9, of which 8 were waited for; matrix products, arithmetic and copies ran while one was open for 4% of the time, Pallas kernels for 0%

commit v1 on v0

v1 whole, which is shorter than its diff:
```python
import math

import jax
import jax.numpy as jnp
from jax import lax
from jax.experimental import pallas as pl
from jax.experimental.pallas import tpu as pltpu
from jax.sharding import PartitionSpec as P

P_SIZE = 64
NS = 128
HEAD_DIMENSION = 128
N_CTX = 32
N_Y = 4
N_Z = 8
N_T = 4
WINDOW = 18

epsilon = 1e-05
rope_base = 500000.0
MESH = pl.DeviceIdType.MESH
VMEM = pltpu.VMEM
DMA = pltpu.SemaphoreType.DMA


def context_peer(index):
    return {"context": index}


def tensor_peer(index):
    return {"tensor": index}


def remote(src, dst, send_sem, recv_sem, peer):
    return pltpu.make_async_remote_copy(
        src_ref=src,
        dst_ref=dst,
        send_sem=send_sem,
        recv_sem=recv_sem,
        device_id=peer,
        device_id_type=MESH,
    )


def barrier_context(me):
    barrier = pltpu.get_barrier_semaphore()

    def signal(step, carry):
        pl.semaphore_signal(
            barrier,
            inc=1,
            device_id=context_peer(lax.rem(me + step, N_CTX)),
            device_id_type=MESH,
        )
        return carry

    lax.fori_loop(1, N_CTX, signal, 0)
    return barrier


def state_kernel(
    pieces, side, incoming, side_out, recv, scanned, send1, recv1, send2, recv2, send3, recv3
):
    me = lax.axis_index("context")
    barrier = barrier_context(me)
    recv[me] = pieces[me]
    side_out[me] = side[me]
    pl.semaphore_wait(barrier, N_CTX - 1)

    def piece_copy(target, slot, step):
        return remote(
            pieces.at[target], recv.at[slot], send1.at[step], recv1.at[slot], context_peer(target)
        )

    def side_copy(target, slot, step):
        return remote(
            side.at[target], side_out.at[slot], send2.at[step], recv2.at[slot], context_peer(target)
        )

    def back_copy(target, slot, step):
        return remote(
            scanned.at[target], incoming.at[slot], send3.at[step], recv3.at[slot], context_peer(target)
        )

    def start_out(step, carry):
        target = lax.rem(me + step, N_CTX)
        side_copy(target, me, step).start()
        piece_copy(target, me, step).start()
        return carry

    lax.fori_loop(1, N_CTX, start_out, 0)

    def arrive(step, carry):
        source = lax.rem(me + step, N_CTX)
        side_copy(source, source, step).wait_recv()
        piece_copy(source, source, step).wait_recv()
        return carry

    lax.fori_loop(1, N_CTX, arrive, 0)

    def one(turn, state):
        scanned[turn] = state.astype(jnp.bfloat16)
        return state * side_out[turn, 2:3, :] + recv[turn].astype(jnp.float32)

    lax.fori_loop(0, N_CTX, one, jnp.zeros(recv.shape[1:], jnp.float32))
    incoming[me] = scanned[me]

    def start_back(step, carry):
        back_copy(lax.rem(me + step, N_CTX), me, step).start()
        return carry

    lax.fori_loop(1, N_CTX, start_back, 0)

    def finish(step, carry):
        source = lax.rem(me + step, N_CTX)
        back_copy(source, source, step).wait_recv()
        piece_copy(source, source, step).wait_send()
        side_copy(source, source, step).wait_send()
        back_copy(source, source, step).wait_send()
        return carry

    lax.fori_loop(1, N_CTX, finish, 0)


def exchange_state(pieces, side):
    shape = pieces.shape
    spec = pl.BlockSpec(memory_space=VMEM)
    return pl.pallas_call(
        state_kernel,
        out_shape=(
            jax.ShapeDtypeStruct(shape, jnp.bfloat16),
            jax.ShapeDtypeStruct(side.shape, jnp.float32),
        ),
        in_specs=[spec, spec],
        out_specs=(spec, spec),
        scratch_shapes=[
            VMEM(shape, jnp.bfloat16),
            VMEM(shape, jnp.bfloat16),
        ]
        + [DMA((N_CTX,))] * 6,
        compiler_params=pltpu.CompilerParams(collective_id=0, has_side_effects=True),
        name="state_exchange",
    )(pieces, side)


def project_kernel(
    normed,
    w_out,
    residual,
    gain,
    weights,
    cosine,
    sine,
    hidden_ref,
    qkv_ref,
    w_tiles,
    relay_a,
    relay_b,
    accum_a,
    accum_b,
    direct_a,
    direct_b,
    stage,
    hold_a,
    hold_b,
    full,
    gathered,
    load_sem,
    rs_send,
    rs_recv,
    ag_send,
    ag_recv,
    z_send,
    z_recv,
    y_send,
    y_recv,
    core_send,
    core_recv,
):
    me = lax.axis_index("tensor")
    place = lax.axis_index("context")
    core = lax.axis_index("dp")
    other = 1 - core
    right = lax.rem(me + 1, N_T)
    left = lax.rem(me + 3, N_T)
    opposite = lax.rem(me + 2, N_T)
    row = lax.div(place, N_Z)
    col = lax.rem(place, N_Z)
    up = lax.rem(row + 1, N_Y)
    down = lax.rem(row + 3, N_Y)
    far = lax.rem(row + 2, N_Y)
    half = normed.shape[0] // 2
    width = residual.shape[1]

    barrier = pltpu.get_barrier_semaphore()
    for peer in (
        tensor_peer(right),
        tensor_peer(left),
        context_peer(up * N_Z + col),
        context_peer(down * N_Z + col),
        {"dp": other},
    ):
        pl.semaphore_signal(barrier, inc=1, device_id=peer, device_id_type=MESH)
    for step in range(1, N_Z):
        pl.semaphore_signal(
            barrier,
            inc=1,
            device_id=context_peer(row * N_Z + lax.rem(col + step, N_Z)),
            device_id_type=MESH,
        )

    order = (opposite, right, left, me)

    def tile_load(number):
        column = pl.multiple_of(order[number] * width, width)
        return pltpu.make_async_copy(
            w_out.at[:, pl.ds(column, width)], w_tiles.at[number], load_sem.at[number]
        )

    for number in range(N_T):
        tile_load(number).start()
    gathered[place, core] = weights[core]

    def multiply(number):
        tile_load(number).wait()
        return jnp.dot(normed[...], w_tiles[number], preferred_element_type=jnp.float32)

    product = multiply(0)
    stage[0] = product[:half].astype(jnp.bfloat16)
    stage[1] = product[half:].astype(jnp.bfloat16)

    pl.semaphore_wait(barrier, 5 + N_Z - 1)

    rs = [
        remote(stage.at[0], relay_a, rs_send.at[0], rs_recv.at[0], tensor_peer(right)),
        remote(stage.at[1], relay_b, rs_send.at[1], rs_recv.at[1], tensor_peer(left)),
        remote(stage.at[2], direct_b, rs_send.at[2], rs_recv.at[2], tensor_peer(right)),
        remote(stage.at[3], direct_a, rs_send.at[3], rs_recv.at[3], tensor_peer(left)),
        remote(stage.at[4], accum_a, rs_send.at[4], rs_recv.at[4], tensor_peer(right)),
        remote(stage.at[5], accum_b, rs_send.at[5], rs_recv.at[5], tensor_peer(left)),
    ]
    rs[0].start()
    rs[1].start()

    def z_copy(step):
        target = row * N_Z + lax.rem(col + step, N_Z)
        return remote(
            weights.at[core],
            gathered.at[place, core],
            z_send.at[step],
            z_recv.at[step],
            context_peer(target),
        )

    for step in (1, 7, 2, 6, 3, 5, 4):
        z_copy(step).start()

    product = multiply(1)
    stage[2] = product[half:].astype(jnp.bfloat16)
    hold_a[...] = product[:half]
    rs[2].start()
    product = multiply(2)
    stage[3] = product[:half].astype(jnp.bfloat16)
    hold_b[...] = product[half:]
    rs[3].start()
    rs[0].wait_recv()
    stage[4] = (hold_a[...] + relay_a[...].astype(jnp.float32)).astype(jnp.bfloat16)
    rs[4].start()
    rs[1].wait_recv()
    stage[5] = (hold_b[...] + relay_b[...].astype(jnp.float32)).astype(jnp.bfloat16)
    rs[5].start()
    product = multiply(3)
    hold_a[...] = product[:half]
    hold_b[...] = product[half:]
    rs[3].wait_recv()
    rs[4].wait_recv()
    hidden_a = (
        residual[:half].astype(jnp.float32)
        + (
            hold_a[...]
            + (direct_a[...].astype(jnp.float32) + accum_a[...].astype(jnp.float32))
        )
    ).astype(jnp.bfloat16)
    full[me, 0] = hidden_a
    hidden_ref[:half] = hidden_a
    rs[2].wait_recv()
    rs[5].wait_recv()
    hidden_b = (
        residual[half:].astype(jnp.float32)
        + (
            hold_b[...]
            + (direct_b[...].astype(jnp.float32) + accum_b[...].astype(jnp.float32))
        )
    ).astype(jnp.bfloat16)
    full[me, 1] = hidden_b
    hidden_ref[half:] = hidden_b

    def full_copy(owner, part, number, target):
        return remote(
            full.at[owner, part],
            full.at[owner, part],
            ag_send.at[number],
            ag_recv.at[number],
            tensor_peer(target),
        )

    full_copy(me, 0, 0, right).start()
    full_copy(me, 1, 3, left).start()
    full_copy(me, 1, 1, right).start()
    full_copy(me, 0, 2, left).start()

    for step in range(1, N_Z):
        z_copy(step).wait_recv()

    def row_copy(owner_row, begin, count, number, target_row):
        return remote(
            gathered.at[pl.ds(owner_row * N_Z + begin, count), core],
            gathered.at[pl.ds(owner_row * N_Z + begin, count), core],
            y_send.at[number],
            y_recv.at[number],
            context_peer(target_row * N_Z + col),
        )

    quarter = N_Z // 2
    row_copy(row, 0, N_Z, 0, up).start()
    row_copy(row, 0, N_Z, 1, down).start()

    def core_copy(owner_row, number):
        return remote(
            gathered.at[pl.ds(owner_row * N_Z, N_Z), core],
            gathered.at[pl.ds(owner_row * N_Z, N_Z), core],
            core_send.at[number],
            core_recv.at[number],
            {"dp": other},
        )

    def core_arrival(owner_row, number):
        return remote(
            gathered.at[pl.ds(owner_row * N_Z, N_Z), other],
            gathered.at[pl.ds(owner_row * N_Z, N_Z), other],
            core_send.at[number],
            core_recv.at[number],
            {"dp": other},
        )

    core_copy(row, 0).start()

    full_copy(left, 0, 0, right).wait_recv()
    full_copy(left, 0, 4, right).start()
    full_copy(right, 1, 3, left).wait_recv()
    full_copy(right, 1, 5, left).start()

    row_copy(down, 0, N_Z, 0, up).wait_recv()
    row_copy(down, 0, quarter, 2, up).start()
    core_copy(down, 1).start()
    row_copy(up, 0, N_Z, 1, down).wait_recv()
    row_copy(up, quarter, quarter, 3, down).start()
    core_copy(up, 2).start()

    full_copy(left, 1, 1, right).wait_recv()
    full_copy(right, 0, 2, left).wait_recv()
    full_copy(opposite, 0, 4, right).wait_recv()
    full_copy(opposite, 1, 5, left).wait_recv()

    row_copy(far, 0, quarter, 2, up).wait_recv()
    row_copy(far, quarter, quarter, 3, down).wait_recv()
    core_copy(far, 3).start()

    core_arrival(row, 0).wait_recv()
    core_arrival(down, 1).wait_recv()
    core_arrival(up, 2).wait_recv()
    core_arrival(far, 3).wait_recv()

    rows_each = gathered.shape[0] // N_T
    depth = rows_each * gathered.shape[1] * gathered.shape[2]
    for part in range(2):
        squares = jnp.zeros((half, 1), jnp.float32)
        for owner in range(N_T):
            stream = full[owner, part].astype(jnp.float32)
            squares = squares + jnp.sum(stream * stream, axis=1, keepdims=True)
        scale = lax.rsqrt(squares / (N_T * width) + epsilon)
        total = jnp.zeros((half, qkv_ref.shape[1]), jnp.float32)
        for owner in range(N_T):
            stream = full[owner, part].astype(jnp.float32)
            block = (stream * scale * gain[:, owner * width : (owner + 1) * width]).astype(
                jnp.bfloat16
            )
            piece = gathered[owner * rows_each : (owner + 1) * rows_each].reshape(
                depth, gathered.shape[3]
            )
            total = total + jnp.dot(block, piece, preferred_element_type=jnp.float32)
        rows = slice(part * half, (part + 1) * half)
        count = total.shape[1] // HEAD_DIMENSION
        for head in range(count):
            lanes = slice(head * HEAD_DIMENSION, (head + 1) * HEAD_DIMENSION)
            value = total[:, lanes]
            if head < count - 1:
                value = value * cosine[rows] + pltpu.roll(value, HEAD_DIMENSION // 2, 1) * sine[rows]
            qkv_ref[rows, lanes] = value.astype(jnp.bfloat16)

    for copy in rs:
        copy.wait_send()
    full_copy(me, 0, 0, right).wait_send()
    full_copy(me, 1, 3, left).wait_send()
    full_copy(me, 1, 1, right).wait_send()
    full_copy(me, 0, 2, left).wait_send()
    full_copy(left, 0, 4, right).wait_send()
    full_copy(right, 1, 5, left).wait_send()
    for step in range(1, N_Z):
        z_copy(step).wait_send()
    row_copy(row, 0, N_Z, 0, up).wait_send()
    row_copy(row, 0, N_Z, 1, down).wait_send()
    row_copy(down, 0, quarter, 2, up).wait_send()
    row_copy(up, quarter, quarter, 3, down).wait_send()
    core_copy(row, 0).wait_send()
    core_copy(down, 1).wait_send()
    core_copy(up, 2).wait_send()
    core_copy(far, 3).wait_send()


def project(normed, w_out, residual, gain, weights, cosine, sine):
    rows, width = residual.shape
    half = rows // 2
    out_width = weights.shape[2]
    spec = pl.BlockSpec(memory_space=VMEM)
    piece = VMEM((half, width), jnp.bfloat16)
    return pl.pallas_call(
        project_kernel,
        out_shape=(
            jax.ShapeDtypeStruct((rows, width), jnp.bfloat16),
            jax.ShapeDtypeStruct((rows, out_width), jnp.bfloat16),
        ),
        in_specs=[spec, pl.BlockSpec(memory_space=pl.ANY)] + [spec] * 5,
        out_specs=(spec, spec),
        scratch_shapes=[
            VMEM((N_T, width, width), jnp.bfloat16),
            piece,
            piece,
            piece,
            piece,
            piece,
            piece,
            VMEM((6, half, width), jnp.bfloat16),
            VMEM((half, width), jnp.float32),
            VMEM((half, width), jnp.float32),
            VMEM((N_T, 2, half, width), jnp.bfloat16),
            VMEM((N_CTX,) + weights.shape, jnp.bfloat16),
            DMA((N_T,)),
            DMA((6,)),
            DMA((6,)),
            DMA((6,)),
            DMA((6,)),
            DMA((N_Z,)),
            DMA((N_Z,)),
            DMA((4,)),
            DMA((4,)),
            DMA((4,)),
            DMA((4,)),
        ],
        compiler_params=pltpu.CompilerParams(
            collective_id=1, has_side_effects=True, vmem_limit_bytes=56 * 1024 * 1024
        ),
        name="project",
    )(normed, w_out, residual, gain, weights, cosine, sine)


def attend_kernel(
    chosen,
    queries,
    keys_values,
    query_docs,
    key_docs,
    out_ref,
    window,
    rows_buf,
    outgoing,
    best_ref,
    denom_ref,
    accum_ref,
    send_sem,
    recv_sem,
    out_send,
    out_recv,
):
    me = lax.axis_index("context")
    barrier = barrier_context(me)
    window[0] = keys_values[...]
    number = queries.shape[0]
    tokens = keys_values.shape[0]
    group = number // tokens
    scale = HEAD_DIMENSION ** (-0.5)

    def attend(slot):
        keys = window[slot, :, :HEAD_DIMENSION]
        values = window[slot, :, HEAD_DIMENSION:]
        scores = scale * lax.dot_general(
            queries[...], keys, (((1,), (1,)), ((), ())), preferred_element_type=jnp.float32
        )
        usable = query_docs[...] == key_docs[slot]
        if slot == 0:
            q_index = lax.broadcasted_iota(jnp.int32, (group, tokens, tokens), 1).reshape(
                number, tokens
            )
            k_index = lax.broadcasted_iota(jnp.int32, (number, tokens), 1)
            usable = usable & (k_index <= q_index)
        scores = jnp.where(usable, scores, -1e30)
        top = jnp.max(scores, axis=1, keepdims=True)
        if slot == 0:
            probs = jnp.exp(scores - top)
            best_ref[...] = jnp.broadcast_to(top, best_ref.shape)
            denom_ref[...] = jnp.broadcast_to(
                jnp.sum(probs, axis=1, keepdims=True), denom_ref.shape
            )
            accum_ref[...] = jnp.dot(
                probs.astype(jnp.bfloat16), values, preferred_element_type=jnp.float32
            )
        else:
            before = best_ref[...]
            fresh = jnp.maximum(before, top)
            fade = jnp.exp(before - fresh)
            probs = jnp.exp(scores - fresh[:, :1])
            best_ref[...] = fresh
            denom_ref[...] = denom_ref[...] * fade + jnp.sum(probs, axis=1, keepdims=True)
            accum_ref[...] = accum_ref[...] * fade + jnp.dot(
                probs.astype(jnp.bfloat16), values, preferred_element_type=jnp.float32
            )

    forward = lax.rem(me + 1, N_CTX)
    backward = lax.rem(me + N_CTX - 1, N_CTX)

    def send(src, dst, sem, target):
        return remote(
            window.at[src], window.at[dst], send_sem.at[sem], recv_sem.at[dst], context_peer(target)
        )

    started = []

    def go(src, dst, target):
        copy = send(src, dst, len(started), target)
        copy.start()
        started.append(copy)

    def arrived(slot):
        remote(
            window.at[slot],
            window.at[slot],
            send_sem.at[0],
            recv_sem.at[slot],
            context_peer(forward),
        ).wait_recv()

    attend(0)
    pl.semaphore_wait(barrier, N_CTX - 1)
    go(0, 8, lax.rem(me + 8, N_CTX))
    go(0, 1, forward)
    go(0, 16, lax.rem(me + 16, N_CTX))

    arrived(8)
    go(8, 9, forward)
    go(8, 7, backward)
    arrived(1)
    go(1, 2, forward)
    attend(8)
    arrived(16)
    go(16, 15, backward)
    go(16, 17, forward)
    attend(1)
    arrived(9)
    go(9, 10, forward)
    arrived(7)
    go(7, 6, backward)
    attend(16)
    arrived(2)
    go(2, 3, forward)
    attend(9)
    arrived(15)
    go(15, 14, backward)
    attend(7)
    attend(2)
    arrived(10)
    go(10, 11, forward)
    arrived(6)
    go(6, 5, backward)
    attend(15)
    arrived(3)
    go(3, 4, forward)
    attend(10)
    arrived(14)
    go(14, 13, backward)
    attend(6)
    attend(3)
    arrived(13)
    go(13, 12, backward)
    attend(14)
    arrived(17)
    attend(17)
    attend(13)
    arrived(11)
    attend(11)
    arrived(5)
    attend(5)
    arrived(4)
    attend(4)
    arrived(12)
    attend(12)

    result = accum_ref[...] / denom_ref[...]
    for head in range(group):
        lanes = slice(head * HEAD_DIMENSION, (head + 1) * HEAD_DIMENSION)
        rows_buf[:, :, lanes] = (
            result[head * tokens : (head + 1) * tokens]
            .reshape(N_CTX, tokens // N_CTX, HEAD_DIMENSION)
            .astype(jnp.bfloat16)
        )

    def place_row(index, carry):
        outgoing[index] = rows_buf[chosen[index]]
        return carry

    lax.fori_loop(0, N_CTX, place_row, 0)
    out_ref[me] = outgoing[me]

    def row_copy(target, slot, step):
        return remote(
            outgoing.at[target],
            out_ref.at[slot],
            out_send.at[step],
            out_recv.at[slot],
            context_peer(target),
        )

    def start_rows(step, carry):
        row_copy(lax.rem(me + step, N_CTX), me, step).start()
        return carry

    lax.fori_loop(1, N_CTX, start_rows, 0)
    for copy in started:
        copy.wait_send()

    def finish(step, carry):
        source = lax.rem(me + step, N_CTX)
        row_copy(source, source, step).wait_recv()
        row_copy(source, source, step).wait_send()
        return carry

    lax.fori_loop(1, N_CTX, finish, 0)


def attend(chosen, queries, keys_values, query_docs, key_docs):
    number = queries.shape[0]
    tokens, pair = keys_values.shape
    out_width = number // tokens * HEAD_DIMENSION
    spec = pl.BlockSpec(memory_space=VMEM)
    rows = (N_CTX, tokens // N_CTX, out_width)
    return pl.pallas_call(
        attend_kernel,
        out_shape=jax.ShapeDtypeStruct(rows, jnp.bfloat16),
        in_specs=[pl.BlockSpec(memory_space=pltpu.SMEM)] + [spec] * 4,
        out_specs=spec,
        scratch_shapes=[
            VMEM((WINDOW, tokens, pair), jnp.bfloat16),
            VMEM(rows, jnp.bfloat16),
            VMEM(rows, jnp.bfloat16),
            VMEM((number, HEAD_DIMENSION), jnp.float32),
            VMEM((number, HEAD_DIMENSION), jnp.float32),
            VMEM((number, HEAD_DIMENSION), jnp.float32),
            DMA((WINDOW,)),
            DMA((WINDOW,)),
            DMA((N_CTX,)),
            DMA((N_CTX,)),
        ],
        compiler_params=pltpu.CompilerParams(
            collective_id=2, has_side_effects=True, vmem_limit_bytes=48 * 1024 * 1024
        ),
        name="attend",
    )(chosen, queries, keys_values, query_docs, key_docs)


def per_device(
    mixer_input,
    gate_z,
    dt_raw,
    dt_bias,
    a_log,
    d_skip,
    conv_weight,
    conv_bias,
    norm_gain,
    w_out,
    residual,
    attn_gain,
    w_query,
    w_key,
    value_weight,
    doc_ids,
    owners,
):
    row_count = mixer_input.shape[0]
    position_here = lax.axis_index("context")
    first_row = position_here * row_count
    lag = conv_weight.shape[0] - 1
    channels = mixer_input.shape[1]
    last_rows = jnp.concatenate(
        [
            mixer_input[row_count - lag :],
            jnp.broadcast_to(
                doc_ids[row_count - lag :, None].astype(jnp.bfloat16), (lag, HEAD_DIMENSION)
            ),
        ],
        axis=1,
    )
    before = lax.ppermute(
        last_rows, "context", [(source, source + 1) for source in range(N_CTX - 1)]
    )
    before_rows = before[:, :channels]
    before_docs = jnp.where(position_here > 0, before[:, channels].astype(jnp.int32), -1)
    prev_doc = before_docs[lag - 1]
    extended = jnp.concatenate([before_rows, mixer_input]).astype(jnp.float32)
    extended_docs = jnp.concatenate([before_docs, doc_ids])
    running = jnp.broadcast_to(conv_bias, mixer_input.shape)
    for offset in range(lag + 1):
        same_doc = extended_docs[offset : offset + row_count] == doc_ids
        running = running + conv_weight[offset] * jnp.where(
            same_doc[:, None], extended[offset : offset + row_count], 0.0
        )
    conv_out = jax.nn.silu(running).astype(jnp.bfloat16)
    heads = dt_raw.shape[1]
    width_x = heads * P_SIZE
    inputs_x = conv_out[:, :width_x].reshape(row_count, heads, P_SIZE)
    in_b = conv_out[:, width_x : width_x + NS]
    out_c = conv_out[:, width_x + NS :]
    step_size = jax.nn.softplus(dt_raw + dt_bias)
    cumul = jnp.cumsum(-step_size * jnp.exp(a_log), axis=0)
    intersection = lax.dot_general(
        out_c, in_b, (((1,), (1,)), ((), ())), preferred_element_type=jnp.float32
    )
    row_ids = jnp.arange(row_count, dtype=jnp.int32)
    allowed = (doc_ids[:, None] == doc_ids[None, :]) & (row_ids[:, None] >= row_ids[None, :])
    decays = jnp.exp(jnp.where(allowed[None], cumul.T[:, :, None] - cumul.T[:, None, :], -jnp.inf))
    weights = decays * intersection[None] * step_size.T[:, None, :]
    inputs_float = inputs_x.astype(jnp.float32)
    outputs = jnp.einsum("hts,shp->thp", weights, inputs_float, precision=lax.Precision.HIGHEST)
    end_weight = (
        jnp.exp(cumul[-1][None, :] - cumul)
        * (doc_ids == doc_ids[-1]).astype(jnp.float32)[:, None]
        * step_size
    )
    state = jnp.einsum(
        "sh,shp,sn->hpn",
        end_weight,
        inputs_float,
        in_b.astype(jnp.float32),
        precision=lax.Precision.HIGHEST,
    )
    through = jnp.exp(cumul[-1]) * (doc_ids[-1] == prev_doc).astype(jnp.float32)

    pieces = state.astype(jnp.bfloat16).reshape(N_CTX, heads * P_SIZE // N_CTX, NS)
    docs_rows = doc_ids.astype(jnp.float32).reshape(row_count // NS, NS)
    side = jnp.concatenate(
        [
            jnp.broadcast_to(docs_rows[None], (N_CTX,) + docs_rows.shape),
            jnp.broadcast_to(
                jnp.repeat(through, N_CTX // heads)[:, None, None],
                (N_CTX, 8 - docs_rows.shape[0], NS),
            ),
        ],
        axis=1,
    )
    incoming_pieces, side_all = exchange_state(pieces, side)
    incoming = incoming_pieces.reshape(heads, P_SIZE, NS)
    all_docs = side_all[:, : docs_rows.shape[0]].reshape(N_CTX, row_count)

    carry_on = (doc_ids == prev_doc).astype(jnp.float32)
    outputs = outputs + jnp.exp(cumul)[:, :, None] * carry_on[:, None, None] * jnp.einsum(
        "tn,hpn->thp", out_c, incoming, preferred_element_type=jnp.float32
    )
    outputs = outputs + d_skip[None, :, None] * inputs_float
    gated = outputs.reshape(row_count, width_x) * jax.nn.silu(gate_z.astype(jnp.float32))
    power = jnp.mean(gated * gated, axis=-1, keepdims=True)
    normed_ssm = (gated * lax.rsqrt(power + epsilon) * norm_gain).astype(jnp.bfloat16)

    shard = jnp.concatenate([w_query, w_key, value_weight], axis=1)
    shard = shard.reshape(2, shard.shape[0] // 2, shard.shape[1])
    positions = first_row + jnp.arange(row_count, dtype=jnp.int32)
    half_width = HEAD_DIMENSION // 2
    freqs = jnp.exp(
        jnp.arange(half_width, dtype=jnp.float32) * (-2.0 * math.log(rope_base) / HEAD_DIMENSION)
    )
    angles = positions.astype(jnp.float32)[:, None] * freqs[None, :]
    cosine = jnp.cos(angles)
    sine = jnp.sin(angles)
    cosine = jnp.concatenate([cosine, cosine], axis=1)
    sine = jnp.concatenate([-sine, sine], axis=1)
    hidden_out, qkv = project(
        normed_ssm, w_out, residual, attn_gain[None, :], shard, cosine, sine
    )
    query_width = w_query.shape[1]
    group = query_width // HEAD_DIMENSION
    queries = (
        qkv[:, :query_width]
        .reshape(row_count, group, HEAD_DIMENSION)
        .transpose(1, 0, 2)
        .reshape(group * row_count, HEAD_DIMENSION)
    )
    device_ids = jnp.arange(N_CTX, dtype=jnp.int32)
    chosen = jnp.sum(
        jnp.where(owners[0][None, :] == device_ids[:, None], device_ids[None, :], 0), axis=1
    )
    blocks = position_here - jnp.arange(WINDOW, dtype=jnp.int32)
    key_docs = jnp.where(
        (blocks >= 0)[:, None], jnp.take(all_docs, jnp.mod(blocks, N_CTX), axis=0), -1.0
    )[:, None, :]
    query_docs = jnp.tile(doc_ids.astype(jnp.float32), group)[:, None]
    attended = attend(chosen, queries, qkv[:, query_width:], query_docs, key_docs)
    return (hidden_out, attended.reshape(row_count, query_width))


def solution(mesh):
    in_specs = (
        P(("dp", "context"), "tensor"),
        P(("dp", "context"), "tensor"),
        P(("dp", "context"), "tensor"),
        P("tensor"),
        P("tensor"),
        P("tensor"),
        P(None, "tensor"),
        P("tensor"),
        P("tensor"),
        P("tensor", None),
        P(("dp", "context"), "tensor"),
        P(),
        P("context", "tensor"),
        P("context", "tensor"),
        P("context", "tensor"),
        P(("dp", "context")),
        P(("dp", "context"), None),
    )
    out_specs = (P(("dp", "context"), "tensor"), P(("dp", "context"), "tensor"))
    return jax.shard_map(
        per_device, mesh=mesh, in_specs=in_specs, out_specs=out_specs, check_vma=False
    )
```

time: 806 us -> 202 us (0.25)
  the two profiles are of different devices: /device:TPU:32 before, /device:TPU:1 now
where the time goes in v1:
time: 202 us; the launch traced here: 198 us
  Pallas kernels  163 us (81%)
  other arithmetic  11.3 us (6%)
  local copies, waits for them, and re-layouts  11.1 us (5%)
  matrix products  5.91 us (3%)
  starting transfers between devices  4.36 us (2%)
  between operations  2.78 us (1%)
    pallas_call x1, Pallas kernels, attend(): pl.pallas_call(attend_kernel, out_shape=jax.ShapeDtypeStruct(rows, jnp.bf...  72.4 us
    pallas_call x1, Pallas kernels, project(): pl.pallas_call(project_kernel, out_shape=(jax.ShapeDtypeStruct((rows, wid...  59.7 us
    pallas_call x1, Pallas kernels, exchange_state(): pl.pallas_call(state_kernel, out_shape=(jax.ShapeDtypeStruct(shape, jnp.b...  30.8 us
    ppermute x1, starting transfers between devices, per_device(): lax.ppermute(last_rows, 'context', [(source, source + 1) for source in ra...  4.36 us
  transfers between devices with their start and end apart: 1, of which 0 were waited for; matrix products, arithmetic and copies ran while one was open for 4% of the time, Pallas kernels for 0%

profile of v1, /device:TPU:1, one launch (start us, length us, event | category | flops | bytes accessed | tf_op | source)
XLA Modules:
  0.0 198.4 jit_solution(3095338995714501010)
XLA Ops:
  0.7 0.8 fusion.46
  1.5 0.1 slice.84
  1.5 0.7 slice.83
  2.4 4.4 %collective-permute-start = (bf16[3,1408]{1,0:T(4,128)(2,1)S(1)}, bf16[3,1408]{1,0:T(4,128)(2,1)S(1)}, u32[]{:S(2)}, u32[]{:S(2)}) collective-permute-start(bf16[3,1408]{1,0:T(4,128)(2,1)S(1)} %pad_maximum_fusion.4), channel_id=1, source_target_pairs={{0,4},{4,8},{8,12},{12,16},{16,20},{20,24},{24,28},{28,32},{32,36}... | collective-permute-start | bytes 25352 | tf_op jit(solution)/shard_map/ppermute | solution.py:712
  6.7 0.9 fusion.29
  7.6 0.9 slice_reduce_fusion.5
  8.6 0.7 exp.36
  9.2 0.8 copy_bitcast_fusion.3
  10.0 0.6 reduce-window.6
  10.6 0.2 slice_reduce_fusion
  10.9 0.2 slice_reduce_fusion.1
  11.1 0.8 select_reduce_fusion.chosen
  11.9 0.5 fusion.37
  12.5 0.8 pad_maximum_fusion.2
  13.3 0.7 pad_maximum_fusion
  14.0 0.6 slice.104
  14.6 0.2 copy.39
  14.9 0.1 convert_select_fusion
  15.0 0.5 slice.102
  15.5 0.1 pad_add_fusion
  16.9 1.4 slice_compare_fusion.2
  18.3 0.1 maximum_convert_fusion
  18.4 1.1 multiply_convert_fusion
  19.6 0.2 fusion.33
  19.8 0.2 copy.29
  20.1 0.1 broadcast_in_dim.146
  20.2 0.1 copy-done.6
  20.3 0.1 multiply_multiply_fusion
  20.4 1.4 convolution_convert_fusion
  21.8 0.1 broadcast_in_dim.147
  21.9 0.7 pad_maximum_fusion.1.side
  22.6 30.8 %state_exchange.1 = (bf16[32,32,128]{2,1,0:T(8,128)(2,1)}, f32[32,8,128]{2,1,0:T(8,128)}) custom-call(bf16[32,32,128]{2,1,0:T(8,128)(2,1)} %bitcast.73, f32[32,8,128]{2,1,0:T(8,128)} %pad_maximum_fusion.1.side), custom_call_target="tpu_custom_call" | custom-call | tf_op jit(solution)/shard_map/state_exchange/pallas_call | solution.py:128
  53.4 3.2 %fusion.12 = f32[256,16,64]{0,2,1:T(8,128)S(1)} fusion(bf16[256,16,64]{0,2,1:T(8,128)(2,1)S(1)} %bitcast.69, f32[16,256]{1,0:T(8,128)S(1)} %get-tuple-element.15, f32[256,256]{1,0:T(8,128)S(1)} %fusion.33, f32[16,256]{1,0:T(8,128)S(1)} %get-tuple-element.18, pred[256,256]{1,0:T(8,128)(4,1)S(1)} %fusion.29), kind=kOutput, calls=%fused_computation.13 | convolution fusion | flops 809500672 | bytes 1933312 | tf_op jit(solution)/shard_map/hts,shp->thp/dot_general | solution.py:742
  56.6 1.2 fusion.16
  57.8 0.3 copy.32
  58.2 0.7 copy-done.1
  58.9 0.4 multiply_reduce_fusion
  59.3 0.3 copy-done.11
  59.5 1.2 multiply_convert_fusion.1.normed
  60.7 59.7 %project.1 = (bf16[256,1024]{1,0:T(8,128)(2,1)}, bf16[256,768]{1,0:T(8,128)(2,1)}) custom-call(bf16[256,1024]{1,0:T(8,128)(2,1)} %multiply_convert_fusion.1.normed, bf16[1024,4096]{1,0:T(8,128)(2,1)} %w_out.1, bf16[256,1024]{1,0:T(8,128)(2,1)} %residual.1, f32[1,4096]{1,0:T(1,128)} %bitcast.77, bf16[2,64,768]{2,1,0:T(8,128)(2,1)} %bitcast.74, ...), custom_call_target="tpu_custom_call" | custom-call | tf_op jit(solution)/shard_map/project/pallas_call | solution.py:427
  120.4 1.1 copy_bitcast_fusion
  121.5 0.9 slice.106.keys_values
  122.4 0.9 slice.107
  123.3 0.6 gather_fusion
  123.9 0.1 broadcast_select_fusion.1.key_docs
  124.0 72.4 %attend.1 = bf16[32,8,512]{2,1,0:T(8,128)(2,1)S(1)} custom-call(s32[32]{0:T(128)S(1)} %select_reduce_fusion.chosen, bf16[1024,128]{1,0:T(8,128)(2,1)S(1)} %bitcast.66, bf16[256,256]{1,0:T(8,128)(2,1)S(1)} %slice.106.keys_values, f32[1024,1]{1,0:T(8,128)S(1)} %bitcast.65, f32[18,1,256]{2,1,0:T(1,128)S(1)} %broadcast_select_fusion.1.key_docs), custom_call_target="tpu_custom_call" | custom-call | tf_op jit(solution)/shard_map/attend/pallas_call | solution.py:655
  196.4 0.8 copy.54
  197.2 0.7 copy.55
  (45 shorter events, 0.5 us)
Async XLA Ops:
  0.6 13.4 %copy-start.9 = (s32[256]{0:T(256)S(1)}, s32[256]{0:T(256)}, u32[]{:S(2)}) copy-start(s32[256]{0:T(256)} %param.32) | copy-start | bytes 3076
  0.6 17.6 %copy-start.2 = (bf16[256,1280]{1,0:T(8,128)(2,1)S(1)}, bf16[256,1280]{1,0:T(8,128)(2,1)}, u32[]{:S(2)}) copy-start(bf16[256,1280]{1,0:T(8,128)(2,1)} %param.17) | copy-start | bytes 1966084
  0.7 12.6 %copy-start.5 = (bf16[128,512]{1,0:T(8,128)(2,1)S(1)}, bf16[128,512]{1,0:T(8,128)(2,1)}, u32[]{:S(2)}) copy-start(bf16[128,512]{1,0:T(8,128)(2,1)} %param.29) | copy-start | bytes 393220
  0.7 12.6 %copy-start.8 = (bf16[128,128]{1,0:T(8,128)(2,1)S(1)}, bf16[128,128]{1,0:T(8,128)(2,1)}, u32[]{:S(2)}) copy-start(bf16[128,128]{1,0:T(8,128)(2,1)} %param.30) | copy-start | bytes 98308
  0.7 12.6 %copy-start.7 = (bf16[128,128]{1,0:T(8,128)(2,1)S(1)}, bf16[128,128]{1,0:T(8,128)(2,1)}, u32[]{:S(2)}) copy-start(bf16[128,128]{1,0:T(8,128)(2,1)} %param.31) | copy-start | bytes 98308
  2.4 12.5 %collective-permute-start = (bf16[3,1408]{1,0:T(4,128)(2,1)S(1)}, bf16[3,1408]{1,0:T(4,128)(2,1)S(1)}, u32[]{:S(2)}, u32[]{:S(2)}) collective-permute-start(bf16[3,1408]{1,0:T(4,128)(2,1)S(1)} %pad_maximum_fusion.4), channel_id=1, source_target_pairs={{0,4},{4,8},{8,12},{12,16},{16,20},{20,24},{24,28},{28,32},{32,36}... | collective-permute-start | bytes 25352 | tf_op jit(solution)/shard_map/ppermute | solution.py:712
  14.0 4.4 %copy-start.10 = (f32[1280]{0:T(1024)S(1)}, f32[1280]{0:T(1024)}, u32[]{:S(2)}) copy-start(f32[1280]{0:T(1024)} %param.24) | copy-start | bytes 15364
  19.6 2.2 %copy-start = (bf16[256,1280]{1,0:T(8,128)(2,1)}, bf16[256,1280]{1,0:T(8,128)(2,1)S(1)}, u32[]{:S(2)}) copy-start(bf16[256,1280]{1,0:T(8,128)(2,1)S(1)} %multiply_convert_fusion) | copy-start | bytes 1966084
  19.6 0.7 copy-start.6
  19.6 0.7 copy-start.12
  53.4 3.2 %copy-start.4 = (bf16[32,32,128]{2,1,0:T(8,128)(2,1)S(1)}, bf16[32,32,128]{2,1,0:T(8,128)(2,1)}, u32[]{:S(2)}) copy-start(bf16[32,32,128]{2,1,0:T(8,128)(2,1)} %get-tuple-element.6) | copy-start | bytes 786436
  53.4 3.2 %copy-start.13 = (f32[16]{0:T(128)S(1)}, f32[16]{0:T(128)}, u32[]{:S(2)}) copy-start(f32[16]{0:T(128)} %param.22) | copy-start | bytes 196
  57.8 1.0 copy-start.1
  58.9 0.7 copy-start.11
  120.4 76.0 %copy-start.3 = (bf16[256,1024]{1,0:T(8,128)(2,1)S(1)}, bf16[256,1024]{1,0:T(8,128)(2,1)}, u32[]{:S(2)}) copy-start(bf16[256,1024]{1,0:T(8,128)(2,1)} %get-tuple-element.38) | copy-start | bytes 1572868

commit v2 on v1

--- a/solution.py
+++ b/solution.py
@@ -15,6 +15,7 @@
 N_Z = 8
 N_T = 4
 WINDOW = 18
+DOCS = 16
 
 epsilon = 1e-05
 rope_base = 500000.0
@@ -152,7 +153,8 @@
     cosine,
     sine,
     hidden_ref,
-    qkv_ref,
+    query_ref,
+    pair_ref,
     w_tiles,
     relay_a,
     relay_b,
@@ -379,7 +381,7 @@
             stream = full[owner, part].astype(jnp.float32)
             squares = squares + jnp.sum(stream * stream, axis=1, keepdims=True)
         scale = lax.rsqrt(squares / (N_T * width) + epsilon)
-        total = jnp.zeros((half, qkv_ref.shape[1]), jnp.float32)
+        total = jnp.zeros((half, weights.shape[2]), jnp.float32)
         for owner in range(N_T):
             stream = full[owner, part].astype(jnp.float32)
             block = (stream * scale * gain[:, owner * width : (owner + 1) * width]).astype(
@@ -396,7 +398,13 @@
             value = total[:, lanes]
             if head < count - 1:
                 value = value * cosine[rows] + pltpu.roll(value, HEAD_DIMENSION // 2, 1) * sine[rows]
-            qkv_ref[rows, lanes] = value.astype(jnp.bfloat16)
+            if head < count - 2:
+                begin = head * 2 * half + part * half
+                query_ref[:, begin : begin + half] = value.T.astype(jnp.bfloat16)
+            elif head < count - 1:
+                pair_ref[rows, :HEAD_DIMENSION] = value.astype(jnp.bfloat16)
+            else:
+                pair_ref[rows, HEAD_DIMENSION:] = value.T.astype(jnp.bfloat16)
 
     for copy in rs:
         copy.wait_send()
@@ -428,10 +436,13 @@
         project_kernel,
         out_shape=(
             jax.ShapeDtypeStruct((rows, width), jnp.bfloat16),
-            jax.ShapeDtypeStruct((rows, out_width), jnp.bfloat16),
+            jax.ShapeDtypeStruct(
+                (HEAD_DIMENSION, rows * (out_width // HEAD_DIMENSION - 2)), jnp.bfloat16
+            ),
+            jax.ShapeDtypeStruct((rows, 2 * HEAD_DIMENSION), jnp.bfloat16),
         ),
         in_specs=[spec, pl.BlockSpec(memory_space=pl.ANY)] + [spec] * 5,
-        out_specs=(spec, spec),
+        out_specs=(spec, spec, spec),
         scratch_shapes=[
             VMEM((N_T, width, width), jnp.bfloat16),
             piece,
@@ -468,8 +479,7 @@
     chosen,
     queries,
     keys_values,
-    query_docs,
-    key_docs,
+    starts,
     out_ref,
     window,
     rows_buf,
@@ -477,7 +487,9 @@
     best_ref,
     denom_ref,
     accum_ref,
-    send_sem,
+    up_send,
+    down_send,
+    far_send,
     recv_sem,
     out_send,
     out_recv,
@@ -485,131 +497,116 @@
     me = lax.axis_index("context")
     barrier = barrier_context(me)
     window[0] = keys_values[...]
-    number = queries.shape[0]
+    number = queries.shape[1]
     tokens = keys_values.shape[0]
     group = number // tokens
-    scale = HEAD_DIMENSION ** (-0.5)
+    scale = HEAD_DIMENSION ** (-0.5) / math.log(2.0)
+
+    def masked_scores(slot):
+        keys = window[slot, :, :HEAD_DIMENSION]
+        scores = scale * jnp.dot(keys, queries[...], preferred_element_type=jnp.float32)
+        key_index = lax.broadcasted_iota(jnp.int32, (tokens, number), 0)
+        usable = key_index >= starts[...] - tokens * (me - slot)
+        return scores, usable, key_index
+
+    def weighted(slot, probs):
+        values = jnp.concatenate(
+            [
+                window[slot, :HEAD_DIMENSION, HEAD_DIMENSION:],
+                window[slot, HEAD_DIMENSION:, HEAD_DIMENSION:],
+            ],
+            axis=1,
+        )
+        return jnp.dot(values, probs.astype(jnp.bfloat16), preferred_element_type=jnp.float32)
+
+    def attend_first():
+        scores, usable, key_index = masked_scores(0)
+        query_index = lax.rem(lax.broadcasted_iota(jnp.int32, (1, number), 1), tokens)
+        scores = jnp.where(usable & (key_index <= query_index), scores, -1e30)
+        top = jnp.max(scores, axis=0, keepdims=True)
+        probs = jnp.exp2(scores - top)
+        best_ref[...] = top
+        denom_ref[...] = jnp.sum(probs, axis=0, keepdims=True)
+        accum_ref[...] = weighted(0, probs)
 
     def attend(slot):
-        keys = window[slot, :, :HEAD_DIMENSION]
-        values = window[slot, :, HEAD_DIMENSION:]
-        scores = scale * lax.dot_general(
-            queries[...], keys, (((1,), (1,)), ((), ())), preferred_element_type=jnp.float32
-        )
-        usable = query_docs[...] == key_docs[slot]
-        if slot == 0:
-            q_index = lax.broadcasted_iota(jnp.int32, (group, tokens, tokens), 1).reshape(
-                number, tokens
-            )
-            k_index = lax.broadcasted_iota(jnp.int32, (number, tokens), 1)
-            usable = usable & (k_index <= q_index)
+        scores, usable, _ = masked_scores(slot)
         scores = jnp.where(usable, scores, -1e30)
-        top = jnp.max(scores, axis=1, keepdims=True)
-        if slot == 0:
-            probs = jnp.exp(scores - top)
-            best_ref[...] = jnp.broadcast_to(top, best_ref.shape)
-            denom_ref[...] = jnp.broadcast_to(
-                jnp.sum(probs, axis=1, keepdims=True), denom_ref.shape
-            )
-            accum_ref[...] = jnp.dot(
-                probs.astype(jnp.bfloat16), values, preferred_element_type=jnp.float32
-            )
-        else:
-            before = best_ref[...]
-            fresh = jnp.maximum(before, top)
-            fade = jnp.exp(before - fresh)
-            probs = jnp.exp(scores - fresh[:, :1])
-            best_ref[...] = fresh
-            denom_ref[...] = denom_ref[...] * fade + jnp.sum(probs, axis=1, keepdims=True)
-            accum_ref[...] = accum_ref[...] * fade + jnp.dot(
-                probs.astype(jnp.bfloat16), values, preferred_element_type=jnp.float32
-            )
+        before = best_ref[...]
+        fresh = jnp.maximum(before, jnp.max(scores, axis=0, keepdims=True))
+        fade = jnp.exp2(before - fresh)
+        probs = jnp.exp2(scores - fresh)
+        best_ref[...] = fresh
+        denom_ref[...] = denom_ref[...] * fade + jnp.sum(probs, axis=0, keepdims=True)
+        accum_ref[...] = accum_ref[...] * fade + weighted(slot, probs)
 
     forward = lax.rem(me + 1, N_CTX)
     backward = lax.rem(me + N_CTX - 1, N_CTX)
 
-    def send(src, dst, sem, target):
-        return remote(
-            window.at[src], window.at[dst], send_sem.at[sem], recv_sem.at[dst], context_peer(target)
-        )
-
-    started = []
-
-    def go(src, dst, target):
-        copy = send(src, dst, len(started), target)
-        copy.start()
-        started.append(copy)
-
-    def arrived(slot):
-        remote(
+    def send_up(slot):
+        return remote(
             window.at[slot],
+            window.at[slot + 1],
+            up_send.at[slot],
+            recv_sem.at[slot + 1],
+            context_peer(forward),
+        )
+
+    def send_down(slot):
+        return remote(
             window.at[slot],
-            send_sem.at[0],
+            window.at[slot - 1],
+            down_send.at[slot],
+            recv_sem.at[slot - 1],
+            context_peer(backward),
+        )
+
+    def send_far(slot):
+        return remote(
+            window.at[0],
+            window.at[slot],
+            far_send.at[slot],
             recv_sem.at[slot],
-            context_peer(forward),
-        ).wait_recv()
-
-    attend(0)
+            context_peer(lax.rem(me + slot, N_CTX)),
+        )
+
+    attend_first()
     pl.semaphore_wait(barrier, N_CTX - 1)
-    go(0, 8, lax.rem(me + 8, N_CTX))
-    go(0, 1, forward)
-    go(0, 16, lax.rem(me + 16, N_CTX))
-
-    arrived(8)
-    go(8, 9, forward)
-    go(8, 7, backward)
-    arrived(1)
-    go(1, 2, forward)
-    attend(8)
-    arrived(16)
-    go(16, 15, backward)
-    go(16, 17, forward)
-    attend(1)
-    arrived(9)
-    go(9, 10, forward)
-    arrived(7)
-    go(7, 6, backward)
-    attend(16)
-    arrived(2)
-    go(2, 3, forward)
-    attend(9)
-    arrived(15)
-    go(15, 14, backward)
-    attend(7)
-    attend(2)
-    arrived(10)
-    go(10, 11, forward)
-    arrived(6)
-    go(6, 5, backward)
-    attend(15)
-    arrived(3)
-    go(3, 4, forward)
-    attend(10)
-    arrived(14)
-    go(14, 13, backward)
-    attend(6)
-    attend(3)
-    arrived(13)
-    go(13, 12, backward)
-    attend(14)
-    arrived(17)
-    attend(17)
-    attend(13)
-    arrived(11)
-    attend(11)
-    arrived(5)
-    attend(5)
-    arrived(4)
-    attend(4)
-    arrived(12)
-    attend(12)
+    send_far(8).start()
+    send_up(0).start()
+    send_far(16).start()
+
+    visits = (8, 1, 16, 9, 7, 2, 15, 10, 6, 3, 14, 17, 13, 11, 5, 4, 12)
+    goes_up = (1, 2, 3, 8, 9, 10, 16)
+    goes_down = (8, 7, 6, 16, 15, 14, 13)
+
+    def visit(step, carry):
+        slot = jnp.int32(visits[0])
+        for number_here, value in enumerate(visits):
+            slot = jnp.where(step == number_here, value, slot)
+        send_far(slot).wait_recv()
+        upward = ((slot >= 1) & (slot <= 3)) | ((slot >= 8) & (slot <= 10)) | (slot == 16)
+        downward = ((slot >= 6) & (slot <= 8)) | ((slot >= 13) & (slot <= 16))
+
+        @pl.when(upward)
+        def _():
+            send_up(slot).start()
+
+        @pl.when(downward)
+        def _():
+            send_down(slot).start()
+
+        attend(slot)
+        return carry
+
+    lax.fori_loop(0, len(visits), visit, 0)
 
     result = accum_ref[...] / denom_ref[...]
     for head in range(group):
         lanes = slice(head * HEAD_DIMENSION, (head + 1) * HEAD_DIMENSION)
         rows_buf[:, :, lanes] = (
-            result[head * tokens : (head + 1) * tokens]
-            .reshape(N_CTX, tokens // N_CTX, HEAD_DIMENSION)
+            result[:, head * tokens : (head + 1) * tokens]
+            .T.reshape(N_CTX, tokens // N_CTX, HEAD_DIMENSION)
             .astype(jnp.bfloat16)
         )
 
@@ -634,8 +631,13 @@
         return carry
 
     lax.fori_loop(1, N_CTX, start_rows, 0)
-    for copy in started:
-        copy.wait_send()
+    send_up(0).wait_send()
+    for slot in goes_up:
+        send_up(slot).wait_send()
+    for slot in goes_down:
+        send_down(slot).wait_send()
+    send_far(8).wait_send()
+    send_far(16).wait_send()
 
     def finish(step, carry):
         source = lax.rem(me + step, N_CTX)
@@ -646,8 +648,8 @@
     lax.fori_loop(1, N_CTX, finish, 0)
 
 
-def attend(chosen, queries, keys_values, query_docs, key_docs):
-    number = queries.shape[0]
+def attend(chosen, queries, keys_values, starts):
+    number = queries.shape[1]
     tokens, pair = keys_values.shape
     out_width = number // tokens * HEAD_DIMENSION
     spec = pl.BlockSpec(memory_space=VMEM)
@@ -655,15 +657,17 @@
     return pl.pallas_call(
         attend_kernel,
         out_shape=jax.ShapeDtypeStruct(rows, jnp.bfloat16),
-        in_specs=[pl.BlockSpec(memory_space=pltpu.SMEM)] + [spec] * 4,
+        in_specs=[pl.BlockSpec(memory_space=pltpu.SMEM)] + [spec] * 3,
         out_specs=spec,
         scratch_shapes=[
             VMEM((WINDOW, tokens, pair), jnp.bfloat16),
             VMEM(rows, jnp.bfloat16),
             VMEM(rows, jnp.bfloat16),
-            VMEM((number, HEAD_DIMENSION), jnp.float32),
-            VMEM((number, HEAD_DIMENSION), jnp.float32),
-            VMEM((number, HEAD_DIMENSION), jnp.float32),
+            VMEM((1, number), jnp.float32),
+            VMEM((1, number), jnp.float32),
+            VMEM((HEAD_DIMENSION, number), jnp.float32),
+            DMA((WINDOW,)),
+            DMA((WINDOW,)),
             DMA((WINDOW,)),
             DMA((WINDOW,)),
             DMA((N_CTX,)),
@@ -673,7 +677,7 @@
             collective_id=2, has_side_effects=True, vmem_limit_bytes=48 * 1024 * 1024
         ),
         name="attend",
-    )(chosen, queries, keys_values, query_docs, key_docs)
+    )(chosen, queries, keys_values, starts)
 
 
 def per_device(
@@ -791,27 +795,26 @@
     sine = jnp.sin(angles)
     cosine = jnp.concatenate([cosine, cosine], axis=1)
     sine = jnp.concatenate([-sine, sine], axis=1)
-    hidden_out, qkv = project(
+    hidden_out, queries, keys_values = project(
         normed_ssm, w_out, residual, attn_gain[None, :], shard, cosine, sine
     )
     query_width = w_query.shape[1]
     group = query_width // HEAD_DIMENSION
-    queries = (
-        qkv[:, :query_width]
-        .reshape(row_count, group, HEAD_DIMENSION)
-        .transpose(1, 0, 2)
-        .reshape(group * row_count, HEAD_DIMENSION)
-    )
     device_ids = jnp.arange(N_CTX, dtype=jnp.int32)
     chosen = jnp.sum(
         jnp.where(owners[0][None, :] == device_ids[:, None], device_ids[None, :], 0), axis=1
     )
-    blocks = position_here - jnp.arange(WINDOW, dtype=jnp.int32)
-    key_docs = jnp.where(
-        (blocks >= 0)[:, None], jnp.take(all_docs, jnp.mod(blocks, N_CTX), axis=0), -1.0
-    )[:, None, :]
-    query_docs = jnp.tile(doc_ids.astype(jnp.float32), group)[:, None]
-    attended = attend(chosen, queries, qkv[:, query_width:], query_docs, key_docs)
+    names = jnp.arange(DOCS, dtype=jnp.int32).astype(jnp.float32)
+    doc_starts = jnp.sum(
+        (all_docs.reshape(1, -1) < names[:, None]).astype(jnp.int32), axis=1
+    )
+    starts = jnp.sum(
+        jnp.where(
+            doc_ids.astype(jnp.float32)[None, :] == names[:, None], doc_starts[:, None], 0
+        ),
+        axis=0,
+    )
+    attended = attend(chosen, queries, keys_values, jnp.tile(starts, group)[None, :])
     return (hidden_out, attended.reshape(row_count, query_width))
 
 

time: 202 us -> 193 us (0.955)
  the two profiles are of different devices: /device:TPU:1 before, /device:TPU:32 now
where the time goes in v2:
time: 193 us; the launch traced here: 190 us
  Pallas kernels  156 us (81%)
  other arithmetic  11.5 us (6%)
  local copies, waits for them, and re-layouts  10.9 us (6%)
  matrix products  5.06 us (3%)
  starting transfers between devices  3.83 us (2%)
  between operations  2.26 us (1%)
    pallas_call x1, Pallas kernels, attend(): pl.pallas_call(attend_kernel, out_shape=jax.ShapeDtypeStruct(rows, jnp.bf...  68.8 us
    pallas_call x1, Pallas kernels, project(): pl.pallas_call(project_kernel, out_shape=(jax.ShapeDtypeStruct((rows, wid...  55.9 us
    pallas_call x1, Pallas kernels, exchange_state(): pl.pallas_call(state_kernel, out_shape=(jax.ShapeDtypeStruct(shape, jnp.b...  31.5 us
    unnamed x32, local copies, waits for them, and re-layouts  5.24 us
  transfers between devices with their start and end apart: 1, of which 0 were waited for; matrix products, arithmetic and copies ran while one was open for 4% of the time, Pallas kernels for 0%

profile of v2, /device:TPU:32, one launch (start us, length us, event | category | flops | bytes accessed | tf_op | source)
XLA Modules:
  0.0 189.9 jit_solution(7723660324259374209)
XLA Ops:
  0.7 0.8 fusion.42
  1.5 0.1 slice.78
  1.5 0.7 slice.77
  2.3 0.1 broadcast_in_dim.127
  2.4 3.8 %collective-permute-start = (bf16[3,1408]{1,0:T(4,128)(2,1)S(1)}, bf16[3,1408]{1,0:T(4,128)(2,1)S(1)}, u32[]{:S(2)}, u32[]{:S(2)}) collective-permute-start(bf16[3,1408]{1,0:T(4,128)(2,1)S(1)} %pad_maximum_fusion.4), channel_id=1, source_target_pairs={{0,4},{4,8},{8,12},{12,16},{16,20},{20,24},{24,28},{28,32},{32,36}... | collective-permute-start | bytes 25352 | tf_op jit(solution)/shard_map/ppermute | solution.py:716
  6.2 0.9 fusion.29
  7.1 0.9 slice_reduce_fusion.5
  8.0 0.7 exp.36
  8.7 0.8 copy_bitcast_fusion.1
  9.5 0.6 reduce-window.6
  10.1 0.2 slice_reduce_fusion
  10.3 0.1 fusion.40
  10.4 0.2 slice_reduce_fusion.1
  10.6 0.8 select_reduce_fusion.1.chosen
  11.3 0.5 fusion.37
  11.9 0.8 pad_maximum_fusion.2
  12.7 0.7 pad_maximum_fusion
  13.4 0.6 slice.98
  14.0 0.1 convert_select_fusion
  14.1 0.5 slice.96
  14.7 0.1 pad_add_fusion
  16.0 1.4 slice_compare_fusion.2
  17.4 0.1 maximum_convert_fusion
  17.6 1.1 multiply_convert_fusion
  18.8 0.2 fusion.33
  19.0 0.2 copy.26
  19.2 0.1 broadcast_in_dim.137
  19.3 0.1 broadcast_in_dim.138
  19.4 0.1 multiply_multiply_fusion
  19.5 1.4 convolution_convert_fusion
  20.9 0.1 broadcast_in_dim.139
  21.0 0.7 pad_maximum_fusion.1.side
  21.7 31.5 %state_exchange.1 = (bf16[32,32,128]{2,1,0:T(8,128)(2,1)}, f32[32,8,128]{2,1,0:T(8,128)}) custom-call(bf16[32,32,128]{2,1,0:T(8,128)(2,1)} %bitcast.57, f32[32,8,128]{2,1,0:T(8,128)} %pad_maximum_fusion.1.side), custom_call_target="tpu_custom_call" | custom-call | tf_op jit(solution)/shard_map/state_exchange/pallas_call | solution.py:129
  53.2 3.2 %fusion.12 = f32[256,16,64]{0,2,1:T(8,128)S(1)} fusion(bf16[256,16,64]{0,2,1:T(8,128)(2,1)S(1)} %bitcast.54, f32[16,256]{1,0:T(8,128)S(1)} %get-tuple-element.17, f32[256,256]{1,0:T(8,128)S(1)} %fusion.33, f32[16,256]{1,0:T(8,128)S(1)} %get-tuple-element.20, pred[256,256]{1,0:T(8,128)(4,1)S(1)} %fusion.29), kind=kOutput, calls=%fused_computation.12 | convolution fusion | flops 809500672 | bytes 1933312 | tf_op jit(solution)/shard_map/hts,shp->thp/dot_general | solution.py:746
  56.4 0.3 fusion.16
  56.8 0.3 copy.29
  57.1 0.7 copy-done.2
  57.8 0.4 multiply_reduce_fusion
  58.2 0.9 slice.99
  59.2 0.3 convert_reduce_fusion
  59.4 0.1 select_reduce_fusion
  59.5 1.2 multiply_convert_fusion.1.normed
  60.7 55.9 %project.1 = (bf16[256,1024]{1,0:T(8,128)(2,1)}, bf16[128,1024]{1,0:T(8,128)(2,1)}, bf16[256,256]{1,0:T(8,128)(2,1)}) custom-call(bf16[256,1024]{1,0:T(8,128)(2,1)} %multiply_convert_fusion.1.normed, bf16[1024,4096]{1,0:T(8,128)(2,1)} %w_out.1, bf16[256,1024]{1,0:T(8,128)(2,1)} %residual.1, f32[1,4096]{1,0:T(1,128)} %bitcast.61, ...), custom_call_target="tpu_custom_call" | custom-call | tf_op jit(solution)/shard_map/project/pallas_call | solution.py:435
  116.6 0.9 copy-done
  117.5 0.9 copy-done.1
  118.4 68.8 %attend.1 = bf16[32,8,512]{2,1,0:T(8,128)(2,1)S(1)} custom-call(s32[32]{0:T(128)S(1)} %select_reduce_fusion.1.chosen, bf16[128,1024]{1,0:T(8,128)(2,1)S(1)} %copy-done, bf16[256,256]{1,0:T(8,128)(2,1)S(1)} %copy-done.1, s32[1,1024]{1,0:T(1,128)S(1)} %bitcast.52), custom_call_target="tpu_custom_call" | custom-call | tf_op jit(solution)/shard_map/attend/pallas_call | solution.py:657
  187.3 1.9 copy.43
  189.2 0.7 copy.44
  (39 shorter events, 0.3 us)
Async XLA Ops:
  0.6 12.8 %copy-start.9 = (s32[256]{0:T(256)S(1)}, s32[256]{0:T(256)}, u32[]{:S(2)}) copy-start(s32[256]{0:T(256)} %param.32) | copy-start | bytes 3076
  0.6 16.8 %copy-start.3 = (bf16[256,1280]{1,0:T(8,128)(2,1)S(1)}, bf16[256,1280]{1,0:T(8,128)(2,1)}, u32[]{:S(2)}) copy-start(bf16[256,1280]{1,0:T(8,128)(2,1)} %param.17) | copy-start | bytes 1966084
  0.7 12.1 %copy-start.5 = (bf16[128,512]{1,0:T(8,128)(2,1)S(1)}, bf16[128,512]{1,0:T(8,128)(2,1)}, u32[]{:S(2)}) copy-start(bf16[128,512]{1,0:T(8,128)(2,1)} %param.29) | copy-start | bytes 393220
  0.7 12.1 %copy-start.8 = (bf16[128,128]{1,0:T(8,128)(2,1)S(1)}, bf16[128,128]{1,0:T(8,128)(2,1)}, u32[]{:S(2)}) copy-start(bf16[128,128]{1,0:T(8,128)(2,1)} %param.30) | copy-start | bytes 98308
  0.7 12.1 %copy-start.7 = (bf16[128,128]{1,0:T(8,128)(2,1)S(1)}, bf16[128,128]{1,0:T(8,128)(2,1)}, u32[]{:S(2)}) copy-start(bf16[128,128]{1,0:T(8,128)(2,1)} %param.31) | copy-start | bytes 98308
  2.4 11.7 %collective-permute-start = (bf16[3,1408]{1,0:T(4,128)(2,1)S(1)}, bf16[3,1408]{1,0:T(4,128)(2,1)S(1)}, u32[]{:S(2)}, u32[]{:S(2)}) collective-permute-start(bf16[3,1408]{1,0:T(4,128)(2,1)S(1)} %pad_maximum_fusion.4), channel_id=1, source_target_pairs={{0,4},{4,8},{8,12},{12,16},{16,20},{20,24},{24,28},{28,32},{32,36}... | collective-permute-start | bytes 25352 | tf_op jit(solution)/shard_map/ppermute | solution.py:716
  12.7 4.8 %copy-start.10 = (f32[1280]{0:T(1024)S(1)}, f32[1280]{0:T(1024)}, u32[]{:S(2)}) copy-start(f32[1280]{0:T(1024)} %param.24) | copy-start | bytes 15364
  18.7 0.7 copy-start.6
  18.7 0.7 copy-start.12
  53.2 3.2 %copy-start.4 = (bf16[32,32,128]{2,1,0:T(8,128)(2,1)S(1)}, bf16[32,32,128]{2,1,0:T(8,128)(2,1)}, u32[]{:S(2)}) copy-start(bf16[32,32,128]{2,1,0:T(8,128)(2,1)} %get-tuple-element.7) | copy-start | bytes 786436
  53.2 3.2 %copy-start.13 = (f32[16]{0:T(128)S(1)}, f32[16]{0:T(128)}, u32[]{:S(2)}) copy-start(f32[16]{0:T(128)} %param.22) | copy-start | bytes 196
  56.8 1.0 copy-start.2
  57.8 1.7 copy-start.11
  116.6 1.0 copy-start
  117.5 0.9 copy-start.1

commit v3 on v2

--- a/solution.py
+++ b/solution.py
@@ -59,89 +59,309 @@
     return barrier
 
 
-def state_kernel(
-    pieces, side, incoming, side_out, recv, scanned, send1, recv1, send2, recv2, send3, recv3
+def softplus(value):
+    return jnp.maximum(value, 0.0) + jnp.log1p(jnp.exp(-jnp.abs(value)))
+
+
+def ssm_kernel(
+    mixer,
+    before,
+    marks,
+    docs_row,
+    docs_tile,
+    gate,
+    dt,
+    dt_turned,
+    bias,
+    bias_turned,
+    rate,
+    rate_turned,
+    skip,
+    taps,
+    conv_bias,
+    gain,
+    shard,
+    normed_ref,
+    side_out,
+    shards_ref,
+    extended,
+    conv,
+    side,
+    pieces,
+    recv,
+    scanned,
+    incoming,
+    base,
+    send1,
+    recv1,
+    send2,
+    recv2,
+    send3,
+    recv3,
+    up_send,
+    up_recv,
+    down_send,
+    down_recv,
 ):
     me = lax.axis_index("context")
+    core = lax.axis_index("dp")
+    row = lax.div(me, N_Z)
+    col = lax.rem(me, N_Z)
+    above = context_peer(row * N_Z + lax.rem(col + 1, N_Z))
+    below = context_peer(row * N_Z + lax.rem(col + N_Z - 1, N_Z))
     barrier = barrier_context(me)
+    rows = mixer.shape[0]
+    channels = mixer.shape[1]
+    heads = dt.shape[1]
+    width = heads * P_SIZE
+    pad = before.shape[0]
+    lag = taps.shape[0] - 1
+    pairs = width // NS
+    exact = lax.Precision.HIGHEST
+
+    extended[:pad] = before[:, :channels].astype(jnp.float32)
+    extended[pad:] = mixer[...].astype(jnp.float32)
+    running = conv_bias[...] + taps[lag : lag + 1] * extended[pad:]
+    for offset in range(lag):
+        begin = pad - lag + offset
+        running = running + taps[offset : offset + 1] * (
+            marks[:, 1 + offset : 2 + offset] * extended[begin : begin + rows]
+        )
+    conv[...] = (running * jax.nn.sigmoid(running)).astype(jnp.bfloat16)
+    in_b = conv[:, width : width + NS]
+    out_c = conv[:, width + NS :]
+
+    first = lax.broadcasted_iota(jnp.int32, (rows, rows), 0)
+    second = lax.broadcasted_iota(jnp.int32, (rows, rows), 1)
+    step = softplus(dt[...] + bias[...])
+    cumul = jnp.dot(
+        jnp.where(first >= second, 1.0, 0.0),
+        -step * jnp.exp(rate[...]),
+        precision=exact,
+        preferred_element_type=jnp.float32,
+    )
+    step_turned = softplus(dt_turned[...] + bias_turned[...])
+    cumul_turned = jnp.dot(
+        -step_turned * jnp.exp(rate_turned[...]),
+        jnp.where(first <= second, 1.0, 0.0),
+        precision=exact,
+        preferred_element_type=jnp.float32,
+    )
+    carry_on = marks[:, 4:5]
+    end_weight = jnp.exp(cumul[rows - 1 : rows] - cumul) * marks[:, 5:6] * step
+    begin_weight = jnp.exp(cumul) * carry_on
+    through = jnp.exp(cumul_turned[:, rows - 1 : rows]) * marks[rows - 1 : rows, 4:5]
+    lower = lax.broadcasted_iota(jnp.int32, (rows, NS), 1) < P_SIZE
+
+    def spread(value, pair):
+        return jnp.where(
+            lower, value[:, 2 * pair : 2 * pair + 1], value[:, 2 * pair + 1 : 2 * pair + 2]
+        )
+
+    each = N_CTX // pairs
+    for pair in range(pairs):
+        lanes = slice(pair * NS, (pair + 1) * NS)
+        scaled = (conv[:, lanes].astype(jnp.float32) * spread(end_weight, pair)).astype(
+            jnp.bfloat16
+        )
+        state = lax.dot_general(
+            scaled, in_b, (((0,), (0,)), ((), ())), preferred_element_type=jnp.float32
+        )
+        pieces[pair * each : (pair + 1) * each] = state.reshape(
+            each, NS // each, NS
+        ).astype(jnp.bfloat16)
+    docs_rows = docs_tile.shape[0]
+    for head in range(heads):
+        tile = jnp.concatenate(
+            [
+                docs_tile[...],
+                jnp.broadcast_to(through[head : head + 1], (8 - docs_rows, NS)),
+            ],
+            axis=0,
+        )
+        for part in range(N_CTX // heads):
+            side[head * (N_CTX // heads) + part] = tile
+
+    def piece_copy(target, slot, number):
+        return remote(
+            pieces.at[target], recv.at[slot], send1.at[number], recv1.at[slot], context_peer(target)
+        )
+
+    def side_copy(target, slot, number):
+        return remote(
+            side.at[target], side_out.at[slot], send2.at[number], recv2.at[slot], context_peer(target)
+        )
+
+    def back_copy(target, slot, number):
+        return remote(
+            scanned.at[target],
+            incoming.at[slot],
+            send3.at[number],
+            recv3.at[slot],
+            context_peer(target),
+        )
+
+    def shard_up(distance):
+        place = lax.rem(col + N_Z - distance, N_Z)
+        return remote(
+            shard.at[core] if distance == 0 else shards_ref.at[place],
+            shards_ref.at[place],
+            up_send.at[distance],
+            up_recv.at[distance],
+            above,
+        )
+
+    def shard_down(distance):
+        place = lax.rem(col + distance, N_Z)
+        return remote(
+            shard.at[core] if distance == 0 else shards_ref.at[place],
+            shards_ref.at[place],
+            down_send.at[distance],
+            down_recv.at[distance],
+            below,
+        )
+
+    pl.semaphore_wait(barrier, N_CTX - 1)
+
+    def start_out(number, carry):
+        target = lax.rem(me + number, N_CTX)
+        side_copy(target, me, number).start()
+        piece_copy(target, me, number).start()
+        return carry
+
+    lax.fori_loop(1, N_CTX, start_out, 0)
+    shard_up(0).start()
+    shard_down(0).start()
     recv[me] = pieces[me]
     side_out[me] = side[me]
-    pl.semaphore_wait(barrier, N_CTX - 1)
-
-    def piece_copy(target, slot, step):
-        return remote(
-            pieces.at[target], recv.at[slot], send1.at[step], recv1.at[slot], context_peer(target)
-        )
-
-    def side_copy(target, slot, step):
-        return remote(
-            side.at[target], side_out.at[slot], send2.at[step], recv2.at[slot], context_peer(target)
-        )
-
-    def back_copy(target, slot, step):
-        return remote(
-            scanned.at[target], incoming.at[slot], send3.at[step], recv3.at[slot], context_peer(target)
-        )
-
-    def start_out(step, carry):
-        target = lax.rem(me + step, N_CTX)
-        side_copy(target, me, step).start()
-        piece_copy(target, me, step).start()
-        return carry
-
-    lax.fori_loop(1, N_CTX, start_out, 0)
-
-    def arrive(step, carry):
-        source = lax.rem(me + step, N_CTX)
-        side_copy(source, source, step).wait_recv()
-        piece_copy(source, source, step).wait_recv()
+    shards_ref[col] = shard[core]
+
+    mixing = lax.dot_general(
+        out_c, in_b, (((1,), (1,)), ((), ())), preferred_element_type=jnp.float32
+    )
+    mixing = jnp.where((first >= second) & (marks[:, 0:1] == docs_row[...]), mixing, 0.0)
+    for pair in range(pairs):
+        lanes = slice(pair * NS, (pair + 1) * NS)
+        inputs = conv[:, lanes]
+        results = []
+        for head in (2 * pair, 2 * pair + 1):
+            fall = jnp.minimum(
+                cumul[:, head : head + 1] - cumul_turned[head : head + 1], 0.0
+            )
+            weight = jnp.exp(fall) * mixing * step_turned[head : head + 1]
+            results.append(
+                jnp.dot(
+                    weight.astype(jnp.bfloat16), inputs, preferred_element_type=jnp.float32
+                )
+            )
+        base[:, lanes] = jnp.where(lower, results[0], results[1]) + skip[
+            :, lanes
+        ] * inputs.astype(jnp.float32)
+
+    def arrive(number, carry):
+        source = lax.rem(me + number, N_CTX)
+        side_copy(source, source, number).wait_recv()
+        piece_copy(source, source, number).wait_recv()
         return carry
 
     lax.fori_loop(1, N_CTX, arrive, 0)
 
     def one(turn, state):
         scanned[turn] = state.astype(jnp.bfloat16)
-        return state * side_out[turn, 2:3, :] + recv[turn].astype(jnp.float32)
+        return state * side_out[turn, docs_rows : docs_rows + 1, :] + recv[turn].astype(
+            jnp.float32
+        )
 
     lax.fori_loop(0, N_CTX, one, jnp.zeros(recv.shape[1:], jnp.float32))
     incoming[me] = scanned[me]
 
-    def start_back(step, carry):
-        back_copy(lax.rem(me + step, N_CTX), me, step).start()
+    def start_back(number, carry):
+        back_copy(lax.rem(me + number, N_CTX), me, number).start()
         return carry
 
     lax.fori_loop(1, N_CTX, start_back, 0)
 
-    def finish(step, carry):
-        source = lax.rem(me + step, N_CTX)
-        back_copy(source, source, step).wait_recv()
-        piece_copy(source, source, step).wait_send()
-        side_copy(source, source, step).wait_send()
-        back_copy(source, source, step).wait_send()
+    def shard_turn(distance):
+        shard_up(distance - 1).wait_recv()
+        shard_up(distance).start()
+        if distance < 3:
+            shard_down(distance - 1).wait_recv()
+            shard_down(distance).start()
+
+    shard_turn(1)
+    gated_by = gate[...].astype(jnp.float32)
+    gated_by = gated_by * jax.nn.sigmoid(gated_by)
+    shard_turn(2)
+
+    def returned(number, carry):
+        source = lax.rem(me + number, N_CTX)
+        back_copy(source, source, number).wait_recv()
         return carry
 
+    lax.fori_loop(1, N_CTX, returned, 0)
+    shard_turn(3)
+    squares = jnp.zeros((rows, 1), jnp.float32)
+    for pair in range(pairs):
+        lanes = slice(pair * NS, (pair + 1) * NS)
+        carried = incoming[pair * each : (pair + 1) * each].reshape(NS, NS)
+        arrived = lax.dot_general(
+            out_c, carried, (((1,), (1,)), ((), ())), preferred_element_type=jnp.float32
+        )
+        gated = (base[:, lanes] + spread(begin_weight, pair) * arrived) * gated_by[:, lanes]
+        base[:, lanes] = gated
+        squares = squares + jnp.sum(gated * gated, axis=1, keepdims=True)
+    scale = lax.rsqrt(squares / width + epsilon)
+    normed_ref[...] = (base[...] * scale * gain[...]).astype(jnp.bfloat16)
+
+    shard_down(2).wait_recv()
+    shard_up(3).wait_recv()
+
+    def finish(number, carry):
+        source = lax.rem(me + number, N_CTX)
+        piece_copy(source, source, number).wait_send()
+        side_copy(source, source, number).wait_send()
+        back_copy(source, source, number).wait_send()
+        return carry
+
     lax.fori_loop(1, N_CTX, finish, 0)
-
-
-def exchange_state(pieces, side):
-    shape = pieces.shape
+    for distance in range(4):
+        shard_up(distance).wait_send()
+        if distance < 3:
+            shard_down(distance).wait_send()
+
+
+def mix(*operands):
+    mixer, dt, shard = operands[0], operands[6], operands[16]
+    rows, channels = mixer.shape
+    width = dt.shape[1] * P_SIZE
+    shape = (N_CTX, width // N_CTX, NS)
     spec = pl.BlockSpec(memory_space=VMEM)
     return pl.pallas_call(
-        state_kernel,
+        ssm_kernel,
         out_shape=(
-            jax.ShapeDtypeStruct(shape, jnp.bfloat16),
-            jax.ShapeDtypeStruct(side.shape, jnp.float32),
+            jax.ShapeDtypeStruct((rows, width), jnp.bfloat16),
+            jax.ShapeDtypeStruct((N_CTX, 8, NS), jnp.float32),
+            jax.ShapeDtypeStruct((N_Z,) + shard.shape[1:], jnp.bfloat16),
         ),
-        in_specs=[spec, spec],
-        out_specs=(spec, spec),
+        in_specs=[spec] * len(operands),
+        out_specs=(spec, spec, spec),
         scratch_shapes=[
+            VMEM((rows + 8, channels), jnp.float32),
+            VMEM((rows, channels), jnp.bfloat16),
+            VMEM((N_CTX, 8, NS), jnp.float32),
             VMEM(shape, jnp.bfloat16),
             VMEM(shape, jnp.bfloat16),
+            VMEM(shape, jnp.bfloat16),
+            VMEM(shape, jnp.bfloat16),
+            VMEM((rows, width), jnp.float32),
         ]
-        + [DMA((N_CTX,))] * 6,
-        compiler_params=pltpu.CompilerParams(collective_id=0, has_side_effects=True),
-        name="state_exchange",
-    )(pieces, side)
+        + [DMA((N_CTX,))] * 6
+        + [DMA((4,))] * 4,
+        compiler_params=pltpu.CompilerParams(
+            collective_id=0, has_side_effects=True, vmem_limit_bytes=48 * 1024 * 1024
+        ),
+        name="mix",
+    )(*operands)
 
 
 def project_kernel(
@@ -172,8 +392,6 @@
     rs_recv,
     ag_send,
     ag_recv,
-    z_send,
-    z_recv,
     y_send,
     y_recv,
     core_send,
@@ -203,14 +421,6 @@
         {"dp": other},
     ):
         pl.semaphore_signal(barrier, inc=1, device_id=peer, device_id_type=MESH)
-    for step in range(1, N_Z):
-        pl.semaphore_signal(
-            barrier,
-            inc=1,
-            device_id=context_peer(row * N_Z + lax.rem(col + step, N_Z)),
-            device_id_type=MESH,
-        )
-
     order = (opposite, right, left, me)
 
     def tile_load(number):
@@ -221,7 +431,7 @@
 
     for number in range(N_T):
         tile_load(number).start()
-    gathered[place, core] = weights[core]
+    gathered[pl.ds(row * N_Z, N_Z), core] = weights[...]
 
     def multiply(number):
         tile_load(number).wait()
@@ -231,7 +441,7 @@
     stage[0] = product[:half].astype(jnp.bfloat16)
     stage[1] = product[half:].astype(jnp.bfloat16)
 
-    pl.semaphore_wait(barrier, 5 + N_Z - 1)
+    pl.semaphore_wait(barrier, 5)
 
     rs = [
         remote(stage.at[0], relay_a, rs_send.at[0], rs_recv.at[0], tensor_peer(right)),
@@ -244,18 +454,38 @@
     rs[0].start()
     rs[1].start()
 
-    def z_copy(step):
-        target = row * N_Z + lax.rem(col + step, N_Z)
-        return remote(
-            weights.at[core],
-            gathered.at[place, core],
-            z_send.at[step],
-            z_recv.at[step],
-            context_peer(target),
-        )
-
-    for step in (1, 7, 2, 6, 3, 5, 4):
-        z_copy(step).start()
+    def row_copy(owner_row, begin, count, number, target_row):
+        return remote(
+            weights if number < 2 else gathered.at[pl.ds(owner_row * N_Z + begin, count), core],
+            gathered.at[pl.ds(owner_row * N_Z + begin, count), core],
+            y_send.at[number],
+            y_recv.at[number],
+            context_peer(target_row * N_Z + col),
+        )
+
+    quarter = N_Z // 2
+    row_copy(row, 0, N_Z, 0, up).start()
+    row_copy(row, 0, N_Z, 1, down).start()
+
+    def core_copy(owner_row, number, source=None):
+        return remote(
+            gathered.at[pl.ds(owner_row * N_Z, N_Z), core] if source is None else source,
+            gathered.at[pl.ds(owner_row * N_Z, N_Z), core],
+            core_send.at[number],
+            core_recv.at[number],
+            {"dp": other},
+        )
+
+    def core_arrival(owner_row, number):
+        return remote(
+            gathered.at[pl.ds(owner_row * N_Z, N_Z), other],
+            gathered.at[pl.ds(owner_row * N_Z, N_Z), other],
+            core_send.at[number],
+            core_recv.at[number],
+            {"dp": other},
+        )
+
+    core_copy(row, 0, weights).start()
 
     product = multiply(1)
     stage[2] = product[half:].astype(jnp.bfloat16)
@@ -310,42 +540,6 @@
     full_copy(me, 1, 3, left).start()
     full_copy(me, 1, 1, right).start()
     full_copy(me, 0, 2, left).start()
-
-    for step in range(1, N_Z):
-        z_copy(step).wait_recv()
-
-    def row_copy(owner_row, begin, count, number, target_row):
-        return remote(
-            gathered.at[pl.ds(owner_row * N_Z + begin, count), core],
-            gathered.at[pl.ds(owner_row * N_Z + begin, count), core],
-            y_send.at[number],
-            y_recv.at[number],
-            context_peer(target_row * N_Z + col),
-        )
-
-    quarter = N_Z // 2
-    row_copy(row, 0, N_Z, 0, up).start()
-    row_copy(row, 0, N_Z, 1, down).start()
-
-    def core_copy(owner_row, number):
-        return remote(
-            gathered.at[pl.ds(owner_row * N_Z, N_Z), core],
-            gathered.at[pl.ds(owner_row * N_Z, N_Z), core],
-            core_send.at[number],
-            core_recv.at[number],
-            {"dp": other},
-        )
-
-    def core_arrival(owner_row, number):
-        return remote(
-            gathered.at[pl.ds(owner_row * N_Z, N_Z), other],
-            gathered.at[pl.ds(owner_row * N_Z, N_Z), other],
-            core_send.at[number],
-            core_recv.at[number],
-            {"dp": other},
-        )
-
-    core_copy(row, 0).start()
 
     full_copy(left, 0, 0, right).wait_recv()
     full_copy(left, 0, 4, right).start()
@@ -402,9 +596,9 @@
                 begin = head * 2 * half + part * half
                 query_ref[:, begin : begin + half] = value.T.astype(jnp.bfloat16)
             elif head < count - 1:
-                pair_ref[rows, :HEAD_DIMENSION] = value.astype(jnp.bfloat16)
+                pair_ref[0, rows] = value.astype(jnp.bfloat16)
             else:
-                pair_ref[rows, HEAD_DIMENSION:] = value.T.astype(jnp.bfloat16)
+                pair_ref[1, rows] = value.T.astype(jnp.bfloat16)
 
     for copy in rs:
         copy.wait_send()
@@ -414,8 +608,6 @@
     full_copy(me, 0, 2, left).wait_send()
     full_copy(left, 0, 4, right).wait_send()
     full_copy(right, 1, 5, left).wait_send()
-    for step in range(1, N_Z):
-        z_copy(step).wait_send()
     row_copy(row, 0, N_Z, 0, up).wait_send()
     row_copy(row, 0, N_Z, 1, down).wait_send()
     row_copy(down, 0, quarter, 2, up).wait_send()
@@ -439,7 +631,7 @@
             jax.ShapeDtypeStruct(
                 (HEAD_DIMENSION, rows * (out_width // HEAD_DIMENSION - 2)), jnp.bfloat16
             ),
-            jax.ShapeDtypeStruct((rows, 2 * HEAD_DIMENSION), jnp.bfloat16),
+            jax.ShapeDtypeStruct((2, rows, HEAD_DIMENSION), jnp.bfloat16),
         ),
         in_specs=[spec, pl.BlockSpec(memory_space=pl.ANY)] + [spec] * 5,
         out_specs=(spec, spec, spec),
@@ -455,14 +647,12 @@
             VMEM((half, width), jnp.float32),
             VMEM((half, width), jnp.float32),
             VMEM((N_T, 2, half, width), jnp.bfloat16),
-            VMEM((N_CTX,) + weights.shape, jnp.bfloat16),
+            VMEM((N_CTX, 2) + weights.shape[1:], jnp.bfloat16),
             DMA((N_T,)),
             DMA((6,)),
             DMA((6,)),
             DMA((6,)),
             DMA((6,)),
-            DMA((N_Z,)),
-            DMA((N_Z,)),
             DMA((4,)),
             DMA((4,)),
             DMA((4,)),
@@ -489,7 +679,7 @@
     accum_ref,
     up_send,
     down_send,
-    far_send,
+    across_send,
     recv_sem,
     out_send,
     out_recv,
@@ -498,12 +688,12 @@
     barrier = barrier_context(me)
     window[0] = keys_values[...]
     number = queries.shape[1]
-    tokens = keys_values.shape[0]
+    tokens = keys_values.shape[1]
     group = number // tokens
     scale = HEAD_DIMENSION ** (-0.5) / math.log(2.0)
 
     def masked_scores(slot):
-        keys = window[slot, :, :HEAD_DIMENSION]
+        keys = window[slot, 0]
         scores = scale * jnp.dot(keys, queries[...], preferred_element_type=jnp.float32)
         key_index = lax.broadcasted_iota(jnp.int32, (tokens, number), 0)
         usable = key_index >= starts[...] - tokens * (me - slot)
@@ -512,8 +702,8 @@
     def weighted(slot, probs):
         values = jnp.concatenate(
             [
-                window[slot, :HEAD_DIMENSION, HEAD_DIMENSION:],
-                window[slot, HEAD_DIMENSION:, HEAD_DIMENSION:],
+                window[slot, 1, :HEAD_DIMENSION],
+                window[slot, 1, HEAD_DIMENSION:],
             ],
             axis=1,
         )
@@ -540,61 +730,82 @@
         denom_ref[...] = denom_ref[...] * fade + jnp.sum(probs, axis=0, keepdims=True)
         accum_ref[...] = accum_ref[...] * fade + weighted(slot, probs)
 
-    forward = lax.rem(me + 1, N_CTX)
+    row = lax.div(me, N_Z)
+    col = lax.rem(me, N_Z)
+    inner = col < N_Z - 1
+    forward = row * N_Z + lax.rem(col + 1, N_Z)
     backward = lax.rem(me + N_CTX - 1, N_CTX)
-
-    def send_up(slot):
-        return remote(
-            window.at[slot],
-            window.at[slot + 1],
-            up_send.at[slot],
-            recv_sem.at[slot + 1],
+    across = lax.rem(me + N_Z, N_CTX)
+    up_base = jnp.where(inner, 0, N_Z)
+    up_shift = jnp.where(inner, 1, 1 - N_Z)
+
+    def send_up(slot, part):
+        return remote(
+            window.at[slot, part],
+            window.at[slot + up_shift, part],
+            up_send.at[slot, part],
+            recv_sem.at[slot + up_shift, part],
             context_peer(forward),
         )
 
-    def send_down(slot):
-        return remote(
-            window.at[slot],
-            window.at[slot - 1],
-            down_send.at[slot],
-            recv_sem.at[slot - 1],
+    def send_down(slot, part):
+        return remote(
+            window.at[slot, part],
+            window.at[slot - 1, part],
+            down_send.at[slot, part],
+            recv_sem.at[slot - 1, part],
             context_peer(backward),
         )
 
-    def send_far(slot):
-        return remote(
-            window.at[0],
-            window.at[slot],
-            far_send.at[slot],
-            recv_sem.at[slot],
-            context_peer(lax.rem(me + slot, N_CTX)),
+    def send_across(slot, part):
+        return remote(
+            window.at[slot, part],
+            window.at[slot + N_Z, part],
+            across_send.at[slot, part],
+            recv_sem.at[slot + N_Z, part],
+            context_peer(across),
         )
 
     attend_first()
     pl.semaphore_wait(barrier, N_CTX - 1)
-    send_far(8).start()
-    send_up(0).start()
-    send_far(16).start()
-
-    visits = (8, 1, 16, 9, 7, 2, 15, 10, 6, 3, 14, 17, 13, 11, 5, 4, 12)
-    goes_up = (1, 2, 3, 8, 9, 10, 16)
-    goes_down = (8, 7, 6, 16, 15, 14, 13)
+    for part in range(2):
+        send_across(0, part).start()
+
+        @pl.when(inner)
+        def _():
+            send_up(0, part).start()
+
+    visits = (8, 1, 7, 16, 9, 2, 6, 15, 10, 3, 14, 5, 17, 11, 13, 4, 12)
+    goes_down = (6, 7, 8, 13, 14, 15, 16)
+    goes_across = (1, 2, 3, 8, 9)
 
     def visit(step, carry):
         slot = jnp.int32(visits[0])
         for number_here, value in enumerate(visits):
             slot = jnp.where(step == number_here, value, slot)
-        send_far(slot).wait_recv()
-        upward = ((slot >= 1) & (slot <= 3)) | ((slot >= 8) & (slot <= 10)) | (slot == 16)
+        upward = (slot >= up_base) & (slot <= up_base + 3)
         downward = ((slot >= 6) & (slot <= 8)) | ((slot >= 13) & (slot <= 16))
-
-        @pl.when(upward)
-        def _():
-            send_up(slot).start()
-
-        @pl.when(downward)
-        def _():
-            send_down(slot).start()
+        crossing = (slot <= 3) | (slot == 8) | (slot == 9)
+        for part in range(2):
+            remote(
+                window.at[slot, part],
+                window.at[slot, part],
+                down_send.at[slot, part],
+                recv_sem.at[slot, part],
+                context_peer(forward),
+            ).wait_recv()
+
+            @pl.when(crossing)
+            def _():
+                send_across(slot, part).start()
+
+            @pl.when(upward)
+            def _():
+                send_up(slot, part).start()
+
+            @pl.when(downward)
+            def _():
+                send_down(slot, part).start()
 
         attend(slot)
         return carry
@@ -631,13 +842,13 @@
         return carry
 
     lax.fori_loop(1, N_CTX, start_rows, 0)
-    send_up(0).wait_send()
-    for slot in goes_up:
-        send_up(slot).wait_send()
-    for slot in goes_down:
-        send_down(slot).wait_send()
-    send_far(8).wait_send()
-    send_far(16).wait_send()
+    for part in range(2):
+        for slot in range(4):
+            send_up(slot + up_base, part).wait_send()
+        for slot in goes_down:
+            send_down(slot, part).wait_send()
+        for slot in (0,) + goes_across:
+            send_across(slot, part).wait_send()
 
     def finish(step, carry):
         source = lax.rem(me + step, N_CTX)
@@ -650,7 +861,7 @@
 
 def attend(chosen, queries, keys_values, starts):
     number = queries.shape[1]
-    tokens, pair = keys_values.shape
+    _, tokens, depth = keys_values.shape
     out_width = number // tokens * HEAD_DIMENSION
     spec = pl.BlockSpec(memory_space=VMEM)
     rows = (N_CTX, tokens // N_CTX, out_width)
@@ -660,16 +871,16 @@
         in_specs=[pl.BlockSpec(memory_space=pltpu.SMEM)] + [spec] * 3,
         out_specs=spec,
         scratch_shapes=[
-            VMEM((WINDOW, tokens, pair), jnp.bfloat16),
+            VMEM((WINDOW, 2, tokens, depth), jnp.bfloat16),
             VMEM(rows, jnp.bfloat16),
             VMEM(rows, jnp.bfloat16),
             VMEM((1, number), jnp.float32),
             VMEM((1, number), jnp.float32),
             VMEM((HEAD_DIMENSION, number), jnp.float32),
-            DMA((WINDOW,)),
-            DMA((WINDOW,)),
-            DMA((WINDOW,)),
-            DMA((WINDOW,)),
+            DMA((WINDOW, 2)),
+            DMA((WINDOW, 2)),
+            DMA((WINDOW, 2)),
+            DMA((WINDOW, 2)),
             DMA((N_CTX,)),
             DMA((N_CTX,)),
         ],
@@ -704,11 +915,12 @@
     first_row = position_here * row_count
     lag = conv_weight.shape[0] - 1
     channels = mixer_input.shape[1]
+    halo = 8
     last_rows = jnp.concatenate(
         [
-            mixer_input[row_count - lag :],
+            mixer_input[row_count - halo :],
             jnp.broadcast_to(
-                doc_ids[row_count - lag :, None].astype(jnp.bfloat16), (lag, HEAD_DIMENSION)
+                doc_ids[row_count - halo :, None].astype(jnp.bfloat16), (halo, HEAD_DIMENSION)
             ),
         ],
         axis=1,
@@ -716,75 +928,47 @@
     before = lax.ppermute(
         last_rows, "context", [(source, source + 1) for source in range(N_CTX - 1)]
     )
-    before_rows = before[:, :channels]
-    before_docs = jnp.where(position_here > 0, before[:, channels].astype(jnp.int32), -1)
-    prev_doc = before_docs[lag - 1]
-    extended = jnp.concatenate([before_rows, mixer_input]).astype(jnp.float32)
-    extended_docs = jnp.concatenate([before_docs, doc_ids])
-    running = jnp.broadcast_to(conv_bias, mixer_input.shape)
-    for offset in range(lag + 1):
-        same_doc = extended_docs[offset : offset + row_count] == doc_ids
-        running = running + conv_weight[offset] * jnp.where(
-            same_doc[:, None], extended[offset : offset + row_count], 0.0
-        )
-    conv_out = jax.nn.silu(running).astype(jnp.bfloat16)
-    heads = dt_raw.shape[1]
-    width_x = heads * P_SIZE
-    inputs_x = conv_out[:, :width_x].reshape(row_count, heads, P_SIZE)
-    in_b = conv_out[:, width_x : width_x + NS]
-    out_c = conv_out[:, width_x + NS :]
-    step_size = jax.nn.softplus(dt_raw + dt_bias)
-    cumul = jnp.cumsum(-step_size * jnp.exp(a_log), axis=0)
-    intersection = lax.dot_general(
-        out_c, in_b, (((1,), (1,)), ((), ())), preferred_element_type=jnp.float32
-    )
-    row_ids = jnp.arange(row_count, dtype=jnp.int32)
-    allowed = (doc_ids[:, None] == doc_ids[None, :]) & (row_ids[:, None] >= row_ids[None, :])
-    decays = jnp.exp(jnp.where(allowed[None], cumul.T[:, :, None] - cumul.T[:, None, :], -jnp.inf))
-    weights = decays * intersection[None] * step_size.T[:, None, :]
-    inputs_float = inputs_x.astype(jnp.float32)
-    outputs = jnp.einsum("hts,shp->thp", weights, inputs_float, precision=lax.Precision.HIGHEST)
-    end_weight = (
-        jnp.exp(cumul[-1][None, :] - cumul)
-        * (doc_ids == doc_ids[-1]).astype(jnp.float32)[:, None]
-        * step_size
-    )
-    state = jnp.einsum(
-        "sh,shp,sn->hpn",
-        end_weight,
-        inputs_float,
-        in_b.astype(jnp.float32),
-        precision=lax.Precision.HIGHEST,
-    )
-    through = jnp.exp(cumul[-1]) * (doc_ids[-1] == prev_doc).astype(jnp.float32)
-
-    pieces = state.astype(jnp.bfloat16).reshape(N_CTX, heads * P_SIZE // N_CTX, NS)
-    docs_rows = doc_ids.astype(jnp.float32).reshape(row_count // NS, NS)
-    side = jnp.concatenate(
-        [
-            jnp.broadcast_to(docs_rows[None], (N_CTX,) + docs_rows.shape),
-            jnp.broadcast_to(
-                jnp.repeat(through, N_CTX // heads)[:, None, None],
-                (N_CTX, 8 - docs_rows.shape[0], NS),
-            ),
+    docs = doc_ids.astype(jnp.float32)
+    before_docs = jnp.where(
+        position_here > 0, before[halo - lag :, channels].astype(jnp.float32), -1.0
+    )
+    extended_docs = jnp.concatenate([before_docs, docs])
+    marks = jnp.stack(
+        [docs]
+        + [
+            (extended_docs[offset : offset + row_count] == docs).astype(jnp.float32)
+            for offset in range(lag)
+        ]
+        + [
+            (docs == before_docs[lag - 1]).astype(jnp.float32),
+            (docs == docs[row_count - 1]).astype(jnp.float32),
         ],
         axis=1,
     )
-    incoming_pieces, side_all = exchange_state(pieces, side)
-    incoming = incoming_pieces.reshape(heads, P_SIZE, NS)
-    all_docs = side_all[:, : docs_rows.shape[0]].reshape(N_CTX, row_count)
-
-    carry_on = (doc_ids == prev_doc).astype(jnp.float32)
-    outputs = outputs + jnp.exp(cumul)[:, :, None] * carry_on[:, None, None] * jnp.einsum(
-        "tn,hpn->thp", out_c, incoming, preferred_element_type=jnp.float32
-    )
-    outputs = outputs + d_skip[None, :, None] * inputs_float
-    gated = outputs.reshape(row_count, width_x) * jax.nn.silu(gate_z.astype(jnp.float32))
-    power = jnp.mean(gated * gated, axis=-1, keepdims=True)
-    normed_ssm = (gated * lax.rsqrt(power + epsilon) * norm_gain).astype(jnp.bfloat16)
-
     shard = jnp.concatenate([w_query, w_key, value_weight], axis=1)
     shard = shard.reshape(2, shard.shape[0] // 2, shard.shape[1])
+    docs_tile = docs.reshape(row_count // NS, NS)
+    normed_ssm, side_all, shards = mix(
+        mixer_input,
+        before,
+        marks,
+        docs[None, :],
+        docs_tile,
+        gate_z,
+        dt_raw,
+        dt_raw.T,
+        dt_bias[None, :],
+        dt_bias[:, None],
+        a_log[None, :],
+        a_log[:, None],
+        jnp.repeat(d_skip, P_SIZE)[None, :],
+        conv_weight,
+        conv_bias[None, :],
+        norm_gain[None, :],
+        shard,
+    )
+    all_docs = side_all[:, : docs_tile.shape[0]].reshape(N_CTX, row_count)
+
     positions = first_row + jnp.arange(row_count, dtype=jnp.int32)
     half_width = HEAD_DIMENSION // 2
     freqs = jnp.exp(
@@ -796,7 +980,7 @@
     cosine = jnp.concatenate([cosine, cosine], axis=1)
     sine = jnp.concatenate([-sine, sine], axis=1)
     hidden_out, queries, keys_values = project(
-        normed_ssm, w_out, residual, attn_gain[None, :], shard, cosine, sine
+        normed_ssm, w_out, residual, attn_gain[None, :], shards, cosine, sine
     )
     query_width = w_query.shape[1]
     group = query_width // HEAD_DIMENSION

time: 193 us -> 164 us (0.85); the launches traced: 190 us -> 163 us
  Pallas kernels: 156 us -> 134 us
  local copies, waits for them, and re-layouts: 10.9 us -> 17.6 us
  other arithmetic: 11.5 us -> 6.39 us
  matrix products: 5.06 us -> 0 us
    pallas_call x1, Pallas kernels: 68.8 us -> 51.7 us  [attend(): pl.pallas_call(attend_kernel, out_shape=jax.ShapeDtypeStruct(rows, jnp.bf...]
    pallas_call x1, Pallas kernels: 55.9 us -> 43.6 us  [project(): pl.pallas_call(project_kernel, out_shape=(jax.ShapeDtypeStruct((rows, wid...]
    pallas_call x1, Pallas kernels: 31.5 us -> 39.1 us  [mix(): pl.pallas_call(ssm_kernel, out_shape=(jax.ShapeDtypeStruct((rows, width),...]
    unnamed x32 -> x27, local copies, waits for them, and re-layouts: 5.24 us -> 12.5 us
    dot_general x4 -> x0, matrix products: 5.06 us -> none  [the longest x1 3.19 us: per_device(): jnp.einsum('hts,shp->thp', weights, inputs_float, precision=lax.Precision...]
    convert_element_type x4 -> x0, other arithmetic: 3.2 us -> none  [the longest x1 1.17 us: per_device(): (gated * lax.rsqrt(power + epsilon) * norm_gain).astype(jnp.bfloat16)]
    broadcast_in_dim x5, local copies, waits for them, and re-layouts: 0.33 us -> 2.96 us  [the longest x1 0.73 us: per_device(): dt_bias[:, None]]
    slice x11 -> x5, local copies, waits for them, and re-layouts: 4.37 us -> 1.9 us  [the longest x1 0.73 us: per_device(): mixer_input[row_count - halo:]]
  transfers between devices with their start and end apart: 1 -> 1, of which waited for: 0 -> 0; matrix products, arithmetic and copies ran while one was open for 4% -> 5% of each run, Pallas kernels for 0% -> 0%
where the time goes in v3:
time: 164 us; the launch traced here: 163 us
  Pallas kernels  134 us (82%)
  local copies, waits for them, and re-layouts  17.6 us (11%)
  other arithmetic  6.39 us (4%)
  starting transfers between devices  3.81 us (2%)
    pallas_call x1, Pallas kernels, attend(): pl.pallas_call(attend_kernel, out_shape=jax.ShapeDtypeStruct(rows, jnp.bf...  51.7 us
    pallas_call x1, Pallas kernels, project(): pl.pallas_call(project_kernel, out_shape=(jax.ShapeDtypeStruct((rows, wid...  43.6 us
    pallas_call x1, Pallas kernels, mix(): pl.pallas_call(ssm_kernel, out_shape=(jax.ShapeDtypeStruct((rows, width),...  39.1 us
    unnamed x27, local copies, waits for them, and re-layouts  12.5 us
    ppermute x1, starting transfers between devices, per_device(): lax.ppermute(last_rows, 'context', [(source, source + 1) for source in ra...  3.81 us
  transfers between devices with their start and end apart: 1, of which 0 were waited for; matrix products, arithmetic and copies ran while one was open for 5% of the time, Pallas kernels for 0%

profile of v3, /device:TPU:32, one launch (start us, length us, event | category | flops | bytes accessed | tf_op | source)
XLA Modules:
  0.0 163.0 jit_solution(5649762633523802144)
XLA Ops:
  0.6 0.8 convert_bitcast_fusion
  1.4 0.1 slice.30
  1.5 0.7 slice.29
  2.2 0.1 broadcast_in_dim.69
  2.3 3.8 %collective-permute-start = (bf16[8,1408]{1,0:T(8,128)(2,1)S(1)}, bf16[8,1408]{1,0:T(8,128)(2,1)S(1)}, u32[]{:S(2)}, u32[]{:S(2)}) collective-permute-start(bf16[8,1408]{1,0:T(8,128)(2,1)S(1)} %pad_maximum_fusion.3), channel_id=1, source_target_pairs={{0,4},{4,8},{8,12},{12,16},{16,20},{20,24},{24,28},{28,32},{32,36}... | collective-permute-start | bytes 67592 | tf_op jit(solution)/shard_map/ppermute | solution.py:928
  6.1 0.8 select_reduce_fusion.1.chosen
  6.9 0.5 fusion
  7.4 1.0 pad_maximum_fusion
  8.4 0.8 pad_maximum_fusion.1
  9.3 0.6 slice.36
  9.8 0.8 copy.36.dt
  10.6 0.7 broadcast_in_dim.76
  11.4 0.1 broadcast_in_dim_reshape.3.skip
  11.5 0.7 copy.37.bias_turned
  12.2 0.7 copy.38.rate_turned
  12.9 0.7 broadcast_in_dim.77.conv_bias
  13.6 0.0 collective-permute-done.before
  13.6 0.1 convert_select_fusion
  13.7 0.1 pad_maximum_fusion.4
  13.8 0.5 slice.35
  14.3 2.0 %compare_convert_fusion.2 = (f32[256]{0:T(256)S(1)}, f32[256]{0:T(256)S(1)}, f32[256]{0:T(256)S(1)}, f32[256]{0:T(256)S(1)}, f32[256]{0:T(256)S(1)}) fusion(f32[259]{0:T(512)S(1)} %pad_maximum_fusion.4, s32[256]{0:T(256)} %param.32, f32[]{:T(128)} %bitcast.6, f32[]{:T(128)} %bitcast.4), kind=kLoop, calls=%fused_computation.16 | loop fusion | flops 2816 | bytes 9224 | tf_op jit(solution)/shard_map/stack | solution.py:936
  16.3 0.1 copy.35.marks
  16.5 0.0 copy-start.1
  16.5 1.1 copy-done.1
  17.6 0.0 copy-start.3
  17.6 1.0 copy-done.3
  18.6 0.0 copy-start.6
  18.6 0.7 copy-done.6
  19.3 0.0 copy-start.7
  19.3 0.7 copy-done.7
  20.0 0.0 copy-start.8
  20.0 0.7 copy-done.8
  20.7 0.0 copy-start.9
  20.7 0.7 copy-done.9
  21.4 0.7 copy-done.10
  22.0 39.1 %mix.1 = (bf16[256,1024]{1,0:T(8,128)(2,1)S(1)}, f32[32,8,128]{2,1,0:T(8,128)S(1)}, bf16[8,64,768]{2,1,0:T(8,128)(2,1)S(1)}) custom-call(bf16[256,1280]{1,0:T(8,128)(2,1)S(1)} %copy-done.1, bf16[8,1408]{1,0:T(8,128)(2,1)S(1)} %collective-permute-done.before, f32[256,6]{1,0:T(8,128)S(1)} %copy.35.marks, f32[1,256]{1,0:T(1,128)S(1)} %bitcast.30, ...), custom_call_target="tpu_custom_call" | custom-call | tf_op jit(solution)/shard_map/mix/pallas_call | solution.py:339
  61.2 0.0 copy-start
  61.2 0.9 copy-done
  62.1 0.8 copy-done.2
  62.9 0.3 convert_reduce_fusion
  63.1 0.1 select_reduce_fusion
  63.2 43.6 %project.1 = (bf16[256,1024]{1,0:T(8,128)(2,1)}, bf16[128,1024]{1,0:T(8,128)(2,1)}, bf16[2,256,128]{2,1,0:T(8,128)(2,1)}) custom-call(bf16[256,1024]{1,0:T(8,128)(2,1)} %copy-done.2, bf16[1024,4096]{1,0:T(8,128)(2,1)} %w_out.1, bf16[256,1024]{1,0:T(8,128)(2,1)} %residual.1, f32[1,4096]{1,0:T(1,128)} %bitcast.38, bf16[8,64,768]{2,1,0:T(8,128)(2,1)} %copy-done, ...), custom_call_target="tpu_custom_call" | custom-call | tf_op jit(solution)/shard_map/project/pallas_call | solution.py:627
  106.9 0.0 copy-start.4
  106.9 0.9 copy-done.4
  107.8 0.9 copy-done.5
  108.7 51.7 %attend.1 = bf16[32,8,512]{2,1,0:T(8,128)(2,1)S(1)} custom-call(s32[32]{0:T(128)S(1)} %select_reduce_fusion.1.chosen, bf16[128,1024]{1,0:T(8,128)(2,1)S(1)} %copy-done.4, bf16[2,256,128]{2,1,0:T(8,128)(2,1)S(1)} %copy-done.5, s32[1,1024]{1,0:T(1,128)S(1)} %bitcast.31), custom_call_target="tpu_custom_call" | custom-call | tf_op jit(solution)/shard_map/attend/pallas_call | solution.py:868
  160.4 1.9 %copy.42 = bf16[256,1024]{1,0:T(8,128)(2,1)} copy(bf16[256,1024]{1,0:T(8,128)(2,1)} %get-tuple-element.31) | data formatting | bytes 1048576
  162.3 0.7 copy.43
  (11 shorter events, 0.1 us)
Async XLA Ops:
  2.3 11.3 %collective-permute-start = (bf16[8,1408]{1,0:T(8,128)(2,1)S(1)}, bf16[8,1408]{1,0:T(8,128)(2,1)S(1)}, u32[]{:S(2)}, u32[]{:S(2)}) collective-permute-start(bf16[8,1408]{1,0:T(8,128)(2,1)S(1)} %pad_maximum_fusion.3), channel_id=1, source_target_pairs={{0,4},{4,8},{8,12},{12,16},{16,20},{20,24},{24,28},{28,32},{32,36}... | collective-permute-start | bytes 67592 | tf_op jit(solution)/shard_map/ppermute | solution.py:928
  16.5 1.1 copy-start.1
  17.6 1.0 copy-start.3
  18.6 0.7 copy-start.6
  19.3 0.7 copy-start.7
  20.0 0.7 copy-start.8
  20.7 0.7 copy-start.9
  21.4 0.7 copy-start.10
  61.2 0.9 copy-start
  62.1 0.8 copy-start.2
  106.9 1.0 copy-start.4
  107.8 0.9 copy-start.5

commit v4 on v0

v4 whole, which is shorter than its diff:
```python
import math
from types import SimpleNamespace

import jax
import jax.numpy as jnp
from jax import lax
from jax.experimental import pallas as pl
from jax.experimental.pallas import tpu as pltpu
from jax.sharding import PartitionSpec as P

P_SIZE = 64
NS = 128
HEAD_DIMENSION = 128
N_CTX = 32
N_Y = 4
N_Z = 8
N_T = 4
WINDOW = 18
DOCS = 16

epsilon = 1e-05
rope_base = 500000.0
MESH = pl.DeviceIdType.MESH
VMEM = pltpu.VMEM
DMA = pltpu.SemaphoreType.DMA


def context_peer(index):
    return {"context": index}


def tensor_peer(index):
    return {"tensor": index}


def remote(src, dst, send_sem, recv_sem, peer):
    return pltpu.make_async_remote_copy(
        src_ref=src,
        dst_ref=dst,
        send_sem=send_sem,
        recv_sem=recv_sem,
        device_id=peer,
        device_id_type=MESH,
    )


def softplus(value):
    return jnp.maximum(value, 0.0) + jnp.log1p(jnp.exp(-jnp.abs(value)))


def around(first, count, step, carry=None):
    lax.fori_loop(first, count, lambda number, none: (step(number), none)[1], 0)


def mix_phase(r, me, core):
    row = lax.div(me, N_Z)
    col = lax.rem(me, N_Z)
    above = context_peer(row * N_Z + lax.rem(col + 1, N_Z))
    below = context_peer(row * N_Z + lax.rem(col + N_Z - 1, N_Z))
    rows, channels = r.mixer.shape
    heads = r.dt.shape[0]
    width = heads * P_SIZE
    pairs = width // NS
    exact = lax.Precision.HIGHEST
    pad = 8
    edge = 16

    r.load_docs.wait()
    r.docs[...] = r.docs_raw[...].astype(jnp.float32)
    docs_row = jnp.concatenate([r.docs[0:1], r.docs[1:2]], axis=1)
    first = lax.broadcasted_iota(jnp.int32, (rows, rows), 0)
    second = lax.broadcasted_iota(jnp.int32, (rows, rows), 1)
    unit = jnp.where(first == second, 1.0, 0.0)
    nt = (((1,), (1,)), ((), ()))

    def turned(value, precision):
        return lax.dot_general(
            unit, value, nt, precision=precision, preferred_element_type=jnp.float32
        )

    docs_col = turned(jnp.broadcast_to(docs_row, (NS, rows)), exact)
    r.docs_ext[pad:] = docs_col

    r.load_taps.wait()
    r.load_conv_bias.wait()
    r.load_mixer.wait()
    r.extended[pad:] = r.mixer[...].astype(jnp.float32)

    def convolve(begin, count):
        here = r.docs_ext[pad + begin : pad + begin + count]
        masks = [
            jnp.where(
                r.docs_ext[pad - 3 + k + begin : pad - 3 + k + begin + count] == here, 1.0, 0.0
            )
            for k in range(3)
        ]
        for chunk in range(channels // NS):
            lanes = slice(chunk * NS, (chunk + 1) * NS)
            running = r.conv_bias[chunk : chunk + 1] + r.taps[3:4, lanes] * (
                r.extended[pad + begin : pad + begin + count, lanes]
            )
            for k in range(3):
                start = pad - 3 + k + begin
                running = running + r.taps[k : k + 1, lanes] * (
                    masks[k] * r.extended[start : start + count, lanes]
                )
            r.conv[begin : begin + count, lanes] = (running * jax.nn.sigmoid(running)).astype(
                jnp.bfloat16
            )

    convolve(edge, rows - edge)

    r.load_dt.wait()
    for small in r.load_small:
        small.wait()
    diagonal = lax.broadcasted_iota(jnp.int32, (heads, heads), 0) == lax.broadcasted_iota(
        jnp.int32, (heads, heads), 1
    )

    def column(ref):
        return jnp.sum(jnp.where(diagonal, ref[...], 0.0), axis=1, keepdims=True)

    bias, rate, skip = column(r.dt_bias), column(r.a_log), column(r.d_skip)
    step_turned = softplus(r.dt[...] + bias)
    cumul_turned = jnp.dot(
        -step_turned * jnp.exp(rate),
        jnp.where(first <= second, 1.0, 0.0),
        precision=exact,
        preferred_element_type=jnp.float32,
    )
    last_doc = docs_row[:, rows - 1 : rows]
    end_turned = (
        jnp.exp(cumul_turned[:, rows - 1 : rows] - cumul_turned)
        * jnp.where(docs_row == last_doc, 1.0, 0.0)
        * step_turned
    )
    cumul = turned(cumul_turned, exact)
    end_weight = turned(end_turned, exact)
    begin_weight = jnp.exp(cumul)
    lower = lax.broadcasted_iota(jnp.int32, (rows, NS), 1) < P_SIZE

    def spread(value, pair):
        return jnp.where(
            lower, value[:, 2 * pair : 2 * pair + 1], value[:, 2 * pair + 1 : 2 * pair + 2]
        )

    pl.semaphore_wait(pltpu.get_barrier_semaphore(), N_CTX - 1 + 3)

    following = context_peer(lax.rem(me + 1, N_CTX))
    halo_rows = remote(
        r.mixer.at[pl.ds(rows - edge, edge)], r.halo, r.halo_send.at[0], r.halo_recv.at[0], following
    )
    halo_docs = remote(
        r.docs_ext.at[pl.ds(rows, pad)],
        r.docs_ext.at[pl.ds(0, pad)],
        r.halo_send.at[1],
        r.halo_recv.at[1],
        following,
    )
    halo_docs.start()
    halo_rows.start()

    def docs_copy(target, slot, number):
        return remote(
            r.docs,
            r.docs_all.at[slot],
            r.docs_send.at[number],
            r.docs_recv.at[slot],
            context_peer(target),
        )

    for load in r.load_shard:
        load.wait()

    def shard_copy(place, distance, sends, recvs, target):
        return remote(
            r.shard if distance == 0 else r.shards.at[place],
            r.shards.at[place],
            sends.at[distance],
            recvs.at[distance],
            target,
        )

    def shard_up(distance):
        place = lax.rem(col + N_Z - distance, N_Z)
        return shard_copy(place, distance, r.up_send, r.up_recv, above)

    def shard_down(distance):
        place = lax.rem(col + distance, N_Z)
        return shard_copy(place, distance, r.down_send, r.down_recv, below)

    halo_docs.wait_recv()
    r.docs_ext[:pad] = jnp.where(me > 0, r.docs_ext[:pad], -1.0)
    halo_rows.wait_recv()
    r.extended[:pad] = r.halo[edge - pad :].astype(jnp.float32)
    convolve(0, edge)
    in_b = r.conv[:, width : width + NS]
    out_c = r.conv[:, width + NS :]
    prev_doc = r.docs_ext[pad - 1 : pad]
    carry_on = jnp.where(r.docs_ext[pad:] == prev_doc, 1.0, 0.0)
    through = jnp.exp(cumul_turned[:, rows - 1 : rows]) * jnp.where(
        last_doc == prev_doc[:, 0:1], 1.0, 0.0
    )

    each = N_CTX // pairs
    for pair in range(pairs):
        lanes = slice(pair * NS, (pair + 1) * NS)
        scaled = (r.conv[:, lanes].astype(jnp.float32) * spread(end_weight, pair)).astype(
            jnp.bfloat16
        )
        state = lax.dot_general(
            scaled, in_b, (((0,), (0,)), ((), ())), preferred_element_type=jnp.float32
        )
        r.pieces[pair * each : (pair + 1) * each] = state.reshape(
            each, NS // each, NS
        ).astype(jnp.bfloat16)
    for head in range(heads):
        for part in range(N_CTX // heads):
            r.side[head * (N_CTX // heads) + part] = jnp.broadcast_to(
                through[head : head + 1], (1, NS)
            )

    def piece_copy(target, slot, number):
        return remote(
            r.pieces.at[target],
            r.recv.at[slot],
            r.send1.at[number],
            r.recv1.at[slot],
            context_peer(target),
        )

    def side_copy(target, slot, number):
        return remote(
            r.side.at[target],
            r.side_all.at[slot],
            r.send2.at[number],
            r.recv2.at[slot],
            context_peer(target),
        )

    def back_copy(target, slot, number):
        return remote(
            r.scanned.at[target],
            r.incoming.at[slot],
            r.send3.at[number],
            r.recv3.at[slot],
            context_peer(target),
        )

    def start_out(number):
        target = lax.rem(me + number, N_CTX)
        side_copy(target, me, number).start()
        piece_copy(target, me, number).start()

    around(1, N_CTX, start_out)
    shard_up(0).start()
    shard_down(0).start()
    around(1, N_CTX, lambda number: docs_copy(lax.rem(me + number, N_CTX), me, number).start())
    r.docs_all[me] = r.docs[...]
    r.recv[me] = r.pieces[me]
    r.side_all[me] = r.side[me]
    r.shards[col] = r.shard[...]

    mixing = lax.dot_general(out_c, in_b, nt, preferred_element_type=jnp.float32)
    docs_wide = jnp.concatenate([docs_col, docs_col], axis=1)
    mixing = jnp.where((first >= second) & (docs_wide == docs_row), mixing, 0.0)
    for pair in range(pairs):
        lanes = slice(pair * NS, (pair + 1) * NS)
        inputs = r.conv[:, lanes]
        results = []
        for head in (2 * pair, 2 * pair + 1):
            fall = jnp.minimum(
                cumul[:, head : head + 1] - cumul_turned[head : head + 1], 0.0
            )
            weight = jnp.exp(fall) * mixing * step_turned[head : head + 1]
            results.append(
                jnp.dot(
                    weight.astype(jnp.bfloat16), inputs, preferred_element_type=jnp.float32
                )
            )
        r.base[:, lanes] = jnp.where(lower, results[0], results[1]) + jnp.where(
            lower[0:1], skip[2 * pair : 2 * pair + 1], skip[2 * pair + 1 : 2 * pair + 2]
        ) * inputs.astype(jnp.float32)

    def arrive(number):
        source = lax.rem(me + number, N_CTX)
        side_copy(source, source, number).wait_recv()
        piece_copy(source, source, number).wait_recv()

    around(1, N_CTX, arrive)

    def one(turn, state):
        r.scanned[turn] = state.astype(jnp.bfloat16)
        return state * r.side_all[turn] + r.recv[turn].astype(
            jnp.float32
        )

    lax.fori_loop(0, N_CTX, one, jnp.zeros(r.recv.shape[1:], jnp.float32))
    r.incoming[me] = r.scanned[me]

    def start_back(number):
        back_copy(lax.rem(me + number, N_CTX), me, number).start()

    around(1, N_CTX, start_back)

    def shard_turn(distance):
        shard_up(distance - 1).wait_recv()
        shard_up(distance).start()
        if distance < 3:
            shard_down(distance - 1).wait_recv()
            shard_down(distance).start()

    shard_turn(1)
    r.load_gate.wait()
    gated_by = r.gate[...].astype(jnp.float32)
    r.swish[...] = gated_by * jax.nn.sigmoid(gated_by)
    shard_turn(2)

    def returned(number):
        source = lax.rem(me + number, N_CTX)
        back_copy(source, source, number).wait_recv()

    around(1, N_CTX, returned)
    shard_turn(3)
    squares = jnp.zeros((rows, 1), jnp.float32)
    for pair in range(pairs):
        lanes = slice(pair * NS, (pair + 1) * NS)
        carried = r.incoming[pair * each : (pair + 1) * each].reshape(NS, NS)
        arrived = lax.dot_general(out_c, carried, nt, preferred_element_type=jnp.float32)
        gated = (
            r.base[:, lanes] + spread(begin_weight, pair) * carry_on * arrived
        ) * r.swish[:, lanes]
        r.base[:, lanes] = gated
        squares = squares + jnp.sum(gated * gated, axis=1, keepdims=True)
    scale = lax.rsqrt(squares / width + epsilon)
    r.load_gain.wait()
    r.normed[...] = (r.base[...] * scale * r.gain[...]).astype(jnp.bfloat16)

    def finish():
        def sent(number):
            source = lax.rem(me + number, N_CTX)
            piece_copy(source, source, number).wait_send()
            side_copy(source, source, number).wait_send()
            docs_copy(source, source, number).wait_send()
            back_copy(source, source, number).wait_send()

        around(1, N_CTX, sent)
        halo_rows.wait_send()
        halo_docs.wait_send()
        for distance in range(4):
            shard_up(distance).wait_send()
            if distance < 3:
                shard_down(distance).wait_send()

    def docs_arrive(number):
        source = lax.rem(me + number, N_CTX)
        docs_copy(source, source, number).wait_recv()

    def shards_arrive():
        shard_down(2).wait_recv()
        shard_up(3).wait_recv()
        around(1, N_CTX, docs_arrive)

    return finish, shards_arrive


def project_phase(r, me_context, core, shards_arrive):
    me = lax.axis_index("tensor")
    place = me_context
    other = 1 - core
    right = lax.rem(me + 1, N_T)
    left = lax.rem(me + 3, N_T)
    opposite = lax.rem(me + 2, N_T)
    row = lax.div(place, N_Z)
    col = lax.rem(place, N_Z)
    up = lax.rem(row + 1, N_Y)
    down = lax.rem(row + 3, N_Y)
    far = lax.rem(row + 2, N_Y)
    width = r.residual.shape[1]
    tokens = r.residual.shape[0]
    half = tokens // 2

    def multiply(number):
        r.load_tiles[number].wait()
        return jnp.dot(r.normed[...], r.w_tiles[number], preferred_element_type=jnp.float32)

    rs = [
        remote(r.stage.at[0], r.relay_a, r.rs_send.at[0], r.rs_recv.at[0], tensor_peer(right)),
        remote(r.stage.at[1], r.relay_b, r.rs_send.at[1], r.rs_recv.at[1], tensor_peer(left)),
        remote(r.stage.at[2], r.direct_b, r.rs_send.at[2], r.rs_recv.at[2], tensor_peer(right)),
        remote(r.stage.at[3], r.direct_a, r.rs_send.at[3], r.rs_recv.at[3], tensor_peer(left)),
        remote(r.stage.at[4], r.accum_a, r.rs_send.at[4], r.rs_recv.at[4], tensor_peer(right)),
        remote(r.stage.at[5], r.accum_b, r.rs_send.at[5], r.rs_recv.at[5], tensor_peer(left)),
    ]
    product = multiply(0)
    r.stage[0] = product[:half].astype(jnp.bfloat16)
    r.stage[1] = product[half:].astype(jnp.bfloat16)
    rs[0].start()
    rs[1].start()

    quarter = N_Z // 2

    def row_copy(owner_row, begin, count, number, target_row):
        part = r.gathered.at[pl.ds(owner_row * N_Z + begin, count), core]
        return remote(
            r.shards if number < 2 else part,
            part,
            r.y_send.at[number],
            r.y_recv.at[number],
            context_peer(target_row * N_Z + col),
        )

    def core_copy(owner_row, number, side=core, source=None):
        part = r.gathered.at[pl.ds(owner_row * N_Z, N_Z), side]
        return remote(
            part if source is None else source,
            part,
            r.core_send.at[number],
            r.core_recv.at[number],
            {"dp": other},
        )

    product = multiply(1)
    r.stage[2] = product[half:].astype(jnp.bfloat16)
    r.hold_a[...] = product[:half]
    rs[2].start()
    product = multiply(2)
    r.stage[3] = product[:half].astype(jnp.bfloat16)
    r.hold_b[...] = product[half:]
    rs[3].start()

    shards_arrive()
    row_copy(row, 0, N_Z, 0, up).start()
    row_copy(row, 0, N_Z, 1, down).start()
    core_copy(row, 0, core, r.shards).start()

    rs[0].wait_recv()
    r.stage[4] = (r.hold_a[...] + r.relay_a[...].astype(jnp.float32)).astype(jnp.bfloat16)
    rs[4].start()
    rs[1].wait_recv()
    r.stage[5] = (r.hold_b[...] + r.relay_b[...].astype(jnp.float32)).astype(jnp.bfloat16)
    rs[5].start()
    product = multiply(3)
    r.hold_a[...] = product[:half]
    r.hold_b[...] = product[half:]
    r.gathered[pl.ds(row * N_Z, N_Z), core] = r.shards[...]

    def full_copy(owner, part, number, target):
        return remote(
            r.full.at[owner, part],
            r.full.at[owner, part],
            r.ag_send.at[number],
            r.ag_recv.at[number],
            tensor_peer(target),
        )

    r.load_residual.wait()
    r.load_attn_gain.wait()
    rs[3].wait_recv()
    rs[4].wait_recv()
    r.full[me, 0] = (
        r.residual[:half].astype(jnp.float32)
        + (
            r.hold_a[...]
            + (r.direct_a[...].astype(jnp.float32) + r.accum_a[...].astype(jnp.float32))
        )
    ).astype(jnp.bfloat16)
    full_copy(me, 0, 0, right).start()
    full_copy(me, 0, 2, left).start()
    rs[2].wait_recv()
    rs[5].wait_recv()
    r.full[me, 1] = (
        r.residual[half:].astype(jnp.float32)
        + (
            r.hold_b[...]
            + (r.direct_b[...].astype(jnp.float32) + r.accum_b[...].astype(jnp.float32))
        )
    ).astype(jnp.bfloat16)
    full_copy(me, 1, 3, left).start()
    full_copy(me, 1, 1, right).start()
    hidden_out = pltpu.make_async_copy(r.full.at[me], r.hidden_ref, r.out_sem.at[0])
    hidden_out.start()

    lane = lax.broadcasted_iota(jnp.int32, (1, HEAD_DIMENSION), 1)
    pair = lax.rem(lane, HEAD_DIMENSION // 2).astype(jnp.float32)
    freqs = jnp.exp(pair * (-2.0 * math.log(rope_base) / HEAD_DIMENSION))
    positions = place * tokens + lax.broadcasted_iota(jnp.int32, (tokens, 1), 0)
    angles = positions.astype(jnp.float32) * freqs
    r.cosine[...] = jnp.cos(angles)
    sine = jnp.sin(angles)
    r.sine[...] = jnp.where(lane < HEAD_DIMENSION // 2, -sine, sine)
    docs_row = jnp.concatenate([r.docs[0:1], r.docs[1:2]], axis=1)
    every = r.docs_all[...]
    starts = jnp.zeros(docs_row.shape, jnp.float32)
    for name in range(1, DOCS):
        count = jnp.sum(jnp.where(every < float(name), 1.0, 0.0), axis=0)
        count = jnp.sum(jnp.sum(count, axis=0, keepdims=True), axis=1, keepdims=True)
        starts = starts + jnp.where(docs_row == float(name), count, 0.0)
    group = r.starts.shape[1] // tokens
    for head in range(group):
        r.starts[:, head * tokens : (head + 1) * tokens] = starts

    full_copy(left, 0, 0, right).wait_recv()
    full_copy(left, 0, 4, right).start()
    full_copy(right, 1, 3, left).wait_recv()
    full_copy(right, 1, 5, left).start()

    row_copy(down, 0, N_Z, 0, up).wait_recv()
    row_copy(down, 0, quarter, 2, up).start()
    core_copy(down, 1).start()
    row_copy(up, 0, N_Z, 1, down).wait_recv()
    row_copy(up, quarter, quarter, 3, down).start()
    core_copy(up, 2).start()

    full_copy(left, 1, 1, right).wait_recv()
    full_copy(right, 0, 2, left).wait_recv()

    row_copy(far, 0, quarter, 2, up).wait_recv()
    row_copy(far, quarter, quarter, 3, down).wait_recv()
    core_copy(far, 3).start()

    full_copy(opposite, 0, 4, right).wait_recv()
    full_copy(opposite, 1, 5, left).wait_recv()
    core_copy(row, 0, other).wait_recv()
    core_copy(down, 1, other).wait_recv()
    core_copy(up, 2, other).wait_recv()
    core_copy(far, 3, other).wait_recv()

    rows_each = r.gathered.shape[0] // N_T
    out_width = r.gathered.shape[3]
    depth = rows_each * r.gathered.shape[1] * r.gathered.shape[2]
    for part in range(2):
        squares = jnp.zeros((half, 1), jnp.float32)
        for owner in range(N_T):
            stream = r.full[owner, part].astype(jnp.float32)
            squares = squares + jnp.sum(stream * stream, axis=1, keepdims=True)
        scale = lax.rsqrt(squares / (N_T * width) + epsilon)
        total = jnp.zeros((half, out_width), jnp.float32)
        for owner in range(N_T):
            stream = r.full[owner, part].astype(jnp.float32)
            gain = jnp.concatenate(
                [
                    r.attn_gain[tile : tile + 1]
                    for tile in range(owner * width // NS, (owner + 1) * width // NS)
                ],
                axis=1,
            )
            block = (stream * scale * gain).astype(jnp.bfloat16)
            piece = r.gathered[owner * rows_each : (owner + 1) * rows_each].reshape(
                depth, out_width
            )
            total = total + jnp.dot(block, piece, preferred_element_type=jnp.float32)
        rows = slice(part * half, (part + 1) * half)
        count = out_width // HEAD_DIMENSION
        for head in range(count):
            lanes = slice(head * HEAD_DIMENSION, (head + 1) * HEAD_DIMENSION)
            value = total[:, lanes]
            if head < count - 1:
                value = (
                    value * r.cosine[rows] + pltpu.roll(value, HEAD_DIMENSION // 2, 1) * r.sine[rows]
                )
            if head < count - 2:
                begin = head * tokens + part * half
                r.queries[:, begin : begin + half] = value.T.astype(jnp.bfloat16)
            elif head < count - 1:
                r.window[0, part] = value.astype(jnp.bfloat16)
            else:
                r.window[0, 2 + part] = value.T.astype(jnp.bfloat16)

    def finish():
        for copy in rs:
            copy.wait_send()
        full_copy(me, 0, 0, right).wait_send()
        full_copy(me, 1, 3, left).wait_send()
        full_copy(me, 1, 1, right).wait_send()
        full_copy(me, 0, 2, left).wait_send()
        full_copy(left, 0, 4, right).wait_send()
        full_copy(right, 1, 5, left).wait_send()
        row_copy(row, 0, N_Z, 0, up).wait_send()
        row_copy(row, 0, N_Z, 1, down).wait_send()
        row_copy(down, 0, quarter, 2, up).wait_send()
        row_copy(up, quarter, quarter, 3, down).wait_send()
        for number, owner in enumerate((row, down, up, far)):
            core_copy(owner, number).wait_send()
        hidden_out.wait()

    return finish


def attend_phase(r, me):
    number = r.queries.shape[1]
    tokens = 2 * r.window.shape[2]
    group = number // tokens
    scale = HEAD_DIMENSION ** (-0.5) / math.log(2.0)
    window = r.window
    def masked_scores(slot):
        keys = window[slot, :2].reshape(tokens, HEAD_DIMENSION)
        scores = scale * jnp.dot(keys, r.queries[...], preferred_element_type=jnp.float32)
        key_index = lax.broadcasted_iota(jnp.int32, (tokens, number), 0).astype(jnp.float32)
        usable = key_index >= (r.starts[...] - (tokens * (me - slot)).astype(jnp.float32))
        return scores, usable, key_index

    def weighted(slot, probs):
        values = jnp.concatenate(
            [
                window[slot, 2],
                window[slot, 3],
            ],
            axis=1,
        )
        return jnp.dot(values, probs.astype(jnp.bfloat16), preferred_element_type=jnp.float32)

    def attend_first():
        scores, usable, key_index = masked_scores(0)
        query_index = lax.rem(lax.broadcasted_iota(jnp.int32, (1, number), 1), tokens)
        query_index = query_index.astype(jnp.float32)
        scores = jnp.where(usable & (key_index <= query_index), scores, -1e30)
        top = jnp.max(scores, axis=0, keepdims=True)
        probs = jnp.exp2(scores - top)
        r.best[...] = top
        r.denom[...] = jnp.sum(probs, axis=0, keepdims=True)
        r.accum[...] = weighted(0, probs)

    def attend(slot):
        scores, usable, _ = masked_scores(slot)
        scores = jnp.where(usable, scores, -1e30)
        before = r.best[...]
        fresh = jnp.maximum(before, jnp.max(scores, axis=0, keepdims=True))
        fade = jnp.exp2(before - fresh)
        probs = jnp.exp2(scores - fresh)
        r.best[...] = fresh
        r.denom[...] = r.denom[...] * fade + jnp.sum(probs, axis=0, keepdims=True)
        r.accum[...] = r.accum[...] * fade + weighted(slot, probs)

    row = lax.div(me, N_Z)
    col = lax.rem(me, N_Z)
    inner = col < N_Z - 1
    forward = row * N_Z + lax.rem(col + 1, N_Z)
    backward = lax.rem(me + N_CTX - 1, N_CTX)
    across = lax.rem(me + N_Z, N_CTX)
    up_base = jnp.where(inner, 0, N_Z)
    up_shift = jnp.where(inner, 1, 1 - N_Z)

    def send_up(slot, part):
        return remote(
            window.at[slot, part],
            window.at[slot + up_shift, part],
            r.win_up_send.at[slot, part],
            r.win_recv_sem.at[slot + up_shift, part],
            context_peer(forward),
        )

    def send_down(slot, part):
        return remote(
            window.at[slot, part],
            window.at[slot - 1, part],
            r.win_down_send.at[slot, part],
            r.win_recv_sem.at[slot - 1, part],
            context_peer(backward),
        )

    def send_across(slot, part):
        return remote(
            window.at[slot, part],
            window.at[slot + N_Z, part],
            r.win_across_send.at[slot, part],
            r.win_recv_sem.at[slot + N_Z, part],
            context_peer(across),
        )

    for part in range(4):
        send_across(0, part).start()

        @pl.when(inner)
        def _():
            send_up(0, part).start()

    attend_first()

    visits = (8, 1, 7, 16, 9, 2, 6, 15, 10, 3, 14, 5, 17, 11, 13, 4, 12)
    goes_down = (6, 7, 8, 13, 14, 15, 16)
    goes_across = (1, 2, 3, 8, 9)

    def visit(step, carry):
        slot = jnp.int32(visits[0])
        for number_here, value in enumerate(visits):
            slot = jnp.where(step == number_here, value, slot)
        upward = (slot >= up_base) & (slot <= up_base + 3)
        downward = ((slot >= 6) & (slot <= 8)) | ((slot >= 13) & (slot <= 16))
        crossing = (slot <= 3) | (slot == 8) | (slot == 9)
        for part in range(4):
            remote(
                window.at[slot, part],
                window.at[slot, part],
                r.win_down_send.at[slot, part],
                r.win_recv_sem.at[slot, part],
                context_peer(forward),
            ).wait_recv()

            @pl.when(crossing)
            def _():
                send_across(slot, part).start()

            @pl.when(upward)
            def _():
                send_up(slot, part).start()

            @pl.when(downward)
            def _():
                send_down(slot, part).start()

        attend(slot)
        return carry

    lax.fori_loop(0, len(visits), visit, 0)

    owner_row = lax.dot_general(
        r.owners[...].astype(jnp.float32),
        jnp.where(
            lax.div(lax.broadcasted_iota(jnp.int32, (N_CTX, tokens), 1), tokens // N_CTX)
            == lax.broadcasted_iota(jnp.int32, (N_CTX, tokens), 0),
            1.0,
            0.0,
        ),
        (((1,), (0,)), ((), ())),
        preferred_element_type=jnp.float32,
    )
    inside = lax.rem(lax.broadcasted_iota(jnp.int32, (1, tokens), 1), tokens // N_CTX)
    target_row = owner_row * (tokens // N_CTX) + inside.astype(jnp.float32)
    order = lax.broadcasted_iota(jnp.int32, (tokens, tokens), 0).astype(jnp.float32)
    chosen = jnp.where(order == target_row, 1.0, 0.0).astype(jnp.bfloat16)
    result = r.accum[...] / r.denom[...]
    for head in range(group):
        lanes = slice(head * HEAD_DIMENSION, (head + 1) * HEAD_DIMENSION)
        context = result[:, head * tokens : (head + 1) * tokens].astype(jnp.bfloat16)
        r.outgoing[:, :, lanes] = (
            lax.dot_general(
                chosen, context, (((1,), (1,)), ((), ())), preferred_element_type=jnp.float32
            )
            .reshape(N_CTX, tokens // N_CTX, HEAD_DIMENSION)
            .astype(jnp.bfloat16)
        )

    def row_copy(target, slot, step):
        return remote(
            r.outgoing.at[target],
            r.out_ref.at[slot],
            r.out_send.at[step],
            r.out_recv.at[slot],
            context_peer(target),
        )

    around(1, N_CTX, lambda step: row_copy(lax.rem(me + step, N_CTX), me, step).start())
    own_rows = pltpu.make_async_copy(r.outgoing.at[me], r.out_ref.at[me], r.out_sem.at[1])
    own_rows.start()
    for part in range(4):
        for slot in range(4):
            send_up(slot + up_base, part).wait_send()
        for slot in goes_down:
            send_down(slot, part).wait_send()
        for slot in (0,) + goes_across:
            send_across(slot, part).wait_send()

    def finish():
        def one(step):
            source = lax.rem(me + step, N_CTX)
            row_copy(source, source, step).wait_recv()
            row_copy(source, source, step).wait_send()

        around(1, N_CTX, one)
        own_rows.wait()

    return finish


def layer(
    mixer,
    gate,
    dt,
    docs,
    taps,
    conv_bias,
    small,
    gain,
    attn_gain,
    w_out,
    residual,
    w_query,
    w_key,
    w_value,
    owners,
):
    rows, channels = mixer.shape
    heads = dt.shape[0]
    width = heads * P_SIZE
    share = residual.shape[1]
    half = rows // 2
    widths = (w_query.shape[1], w_key.shape[1], w_value.shape[1])
    total_width = sum(widths)
    shard_rows = w_query.shape[0] // 2
    group = widths[0] // HEAD_DIMENSION
    out_rows = (N_CTX, rows // N_CTX, widths[0])
    bf, f32 = jnp.bfloat16, jnp.float32
    state = (N_CTX, width // N_CTX, NS)
    piece = VMEM((half, share), bf)
    scratch = dict(
        mixer=VMEM(mixer.shape, bf),
        gate=VMEM(gate.shape, bf),
        dt=VMEM(dt.shape, f32),
        docs=VMEM(docs.shape, f32),
        docs_raw=VMEM(docs.shape, jnp.int32),
        taps=VMEM(taps.shape, f32),
        conv_bias=VMEM(conv_bias.shape, f32),
        dt_bias=VMEM((1, heads), f32),
        a_log=VMEM((1, heads), f32),
        d_skip=VMEM((1, heads), f32),
        gain=VMEM(gain.shape, f32),
        attn_gain=VMEM(attn_gain.shape, f32),
        residual=VMEM(residual.shape, bf),
        owners=VMEM(owners.shape, jnp.int32),
        shard=VMEM((shard_rows, total_width), bf),
        w_tiles=VMEM((N_T, w_out.shape[0], share), bf),
        load_sem=DMA((16,)),
        tile_sem=DMA((N_T,)),
        out_sem=DMA((2,)),
        extended=VMEM((rows + 8, channels), f32),
        docs_ext=VMEM((rows + 8, NS), f32),
        halo=VMEM((16, channels), bf),
        halo_send=DMA((2,)),
        halo_recv=DMA((2,)),
        conv=VMEM((rows, channels), bf),
        side=VMEM((N_CTX, 1, NS), f32),
        side_all=VMEM((N_CTX, 1, NS), f32),
        docs_all=VMEM((N_CTX,) + docs.shape, f32),
        docs_send=DMA((N_CTX,)),
        docs_recv=DMA((N_CTX,)),
        pieces=VMEM(state, bf),
        recv=VMEM(state, bf),
        scanned=VMEM(state, bf),
        incoming=VMEM(state, bf),
        base=VMEM((rows, width), f32),
        swish=VMEM((rows, width), f32),
        normed=VMEM((rows, width), bf),
        shards=VMEM((N_Z, shard_rows, total_width), bf),
        send1=DMA((N_CTX,)),
        recv1=DMA((N_CTX,)),
        send2=DMA((N_CTX,)),
        recv2=DMA((N_CTX,)),
        send3=DMA((N_CTX,)),
        recv3=DMA((N_CTX,)),
        up_send=DMA((4,)),
        up_recv=DMA((4,)),
        down_send=DMA((4,)),
        down_recv=DMA((4,)),
        relay_a=piece,
        relay_b=piece,
        accum_a=piece,
        accum_b=piece,
        direct_a=piece,
        direct_b=piece,
        stage=VMEM((6, half, share), bf),
        hold_a=VMEM((half, share), f32),
        hold_b=VMEM((half, share), f32),
        full=VMEM((N_T, 2, half, share), bf),
        gathered=VMEM((N_CTX, 2, shard_rows, total_width), bf),
        cosine=VMEM((rows, HEAD_DIMENSION), f32),
        sine=VMEM((rows, HEAD_DIMENSION), f32),
        starts=VMEM((1, group * rows), f32),
        rs_send=DMA((6,)),
        rs_recv=DMA((6,)),
        ag_send=DMA((6,)),
        ag_recv=DMA((6,)),
        y_send=DMA((4,)),
        y_recv=DMA((4,)),
        core_send=DMA((4,)),
        core_recv=DMA((4,)),
        queries=VMEM((HEAD_DIMENSION, group * rows), bf),
        window=VMEM((WINDOW, 4, half, HEAD_DIMENSION), bf),
        outgoing=VMEM(out_rows, bf),
        best=VMEM((1, group * rows), f32),
        denom=VMEM((1, group * rows), f32),
        accum=VMEM((HEAD_DIMENSION, group * rows), f32),
        win_up_send=DMA((WINDOW, 4)),
        win_down_send=DMA((WINDOW, 4)),
        win_across_send=DMA((WINDOW, 4)),
        win_recv_sem=DMA((WINDOW, 4)),
        out_send=DMA((N_CTX,)),
        out_recv=DMA((N_CTX,)),
    )
    names = [
        "mixer_in",
        "gate_in",
        "dt_in",
        "docs_in",
        "taps_in",
        "conv_bias_in",
        "dt_bias_in",
        "a_log_in",
        "d_skip_in",
        "gain_in",
        "attn_gain_in",
        "w_out",
        "residual_in",
        "w_query",
        "w_key",
        "w_value",
        "owners_in",
        "hidden_ref",
        "out_ref",
    ] + list(scratch)

    def kernel(*refs):
        r = SimpleNamespace(**dict(zip(names, refs)))
        me = lax.axis_index("context")
        here = lax.axis_index("tensor")
        core = lax.axis_index("dp")
        barrier = pltpu.get_barrier_semaphore()

        def signal(peer):
            pl.semaphore_signal(barrier, inc=1, device_id=peer, device_id_type=MESH)

        around(1, N_CTX, lambda step: signal(context_peer(lax.rem(me + step, N_CTX))))
        signal(tensor_peer(lax.rem(here + 1, N_T)))
        signal(tensor_peer(lax.rem(here + 3, N_T)))
        signal({"dp": 1 - core})

        def load(src, dst, number):
            copy = pltpu.make_async_copy(src, dst, r.load_sem.at[number])
            copy.start()
            return copy

        r.load_docs = load(r.docs_in, r.docs_raw, 0)
        r.load_taps = load(r.taps_in, r.taps, 1)
        r.load_conv_bias = load(r.conv_bias_in, r.conv_bias, 10)
        r.load_small = [
            load(r.dt_bias_in, r.dt_bias, 11),
            load(r.a_log_in, r.a_log, 12),
            load(r.d_skip_in, r.d_skip, 13),
        ]
        r.load_mixer = load(r.mixer_in, r.mixer, 2)
        r.load_dt = load(r.dt_in, r.dt, 3)
        half_rows = pl.ds(core * shard_rows, shard_rows)
        r.load_shard = []
        begin = 0
        for number, (source, count) in enumerate(zip((r.w_query, r.w_key, r.w_value), widths)):
            r.load_shard.append(
                load(source.at[half_rows], r.shard.at[:, pl.ds(begin, count)], 4 + number)
            )
            begin += count
        r.load_gate = load(r.gate_in, r.gate, 7)
        r.load_gain = load(r.gain_in, r.gain, 14)
        r.load_attn_gain = load(r.attn_gain_in, r.attn_gain, 15)
        r.load_residual = load(r.residual_in, r.residual, 8)
        load_owners = load(r.owners_in, r.owners, 9)
        r.load_tiles = []
        for number, owner in enumerate((here + 2, here + 1, here + 3, here)):
            column = pl.multiple_of(lax.rem(owner, N_T) * share, share)
            copy = pltpu.make_async_copy(
                r.w_out.at[:, pl.ds(column, share)], r.w_tiles.at[number], r.tile_sem.at[number]
            )
            copy.start()
            r.load_tiles.append(copy)

        finish_mix, shards_arrive = mix_phase(r, me, core)
        finish_project = project_phase(r, me, core, shards_arrive)
        load_owners.wait()
        finish_attend = attend_phase(r, me)
        finish_mix()
        finish_project()
        finish_attend()

    anywhere = pl.BlockSpec(memory_space=pl.ANY)
    return pl.pallas_call(
        kernel,
        out_shape=(
            jax.ShapeDtypeStruct((2, half, share), bf),
            jax.ShapeDtypeStruct(out_rows, bf),
        ),
        in_specs=[anywhere] * 17,
        out_specs=(anywhere, anywhere),
        scratch_shapes=list(scratch.values()),
        compiler_params=pltpu.CompilerParams(
            collective_id=0, has_side_effects=True, vmem_limit_bytes=60 * 1024 * 1024
        ),
        name="layer",
    )(
        mixer,
        gate,
        dt,
        docs,
        taps,
        conv_bias,
        *small,
        gain,
        attn_gain,
        w_out,
        residual,
        w_query,
        w_key,
        w_value,
        owners,
    )


def per_device(
    mixer_input,
    gate_z,
    dt_raw,
    dt_bias,
    a_log,
    d_skip,
    conv_weight,
    conv_bias,
    norm_gain,
    w_out,
    residual,
    attn_gain,
    w_query,
    w_key,
    value_weight,
    doc_ids,
    owners,
):
    row_count, channels = mixer_input.shape
    share = residual.shape[1]

    hidden_out, attended = layer(
        mixer_input,
        gate_z,
        dt_raw.T,
        doc_ids.reshape(row_count // NS, NS),
        conv_weight,
        conv_bias.reshape(channels // NS, NS),
        (dt_bias[None, :], a_log[None, :], d_skip[None, :]),
        norm_gain[None, :],
        attn_gain.reshape(-1, NS),
        w_out,
        residual,
        w_query,
        w_key,
        value_weight,
        owners,
    )
    return (
        hidden_out.reshape(row_count, share),
        attended.reshape(row_count, w_query.shape[1]),
    )


def solution(mesh):
    in_specs = (
        P(("dp", "context"), "tensor"),
        P(("dp", "context"), "tensor"),
        P(("dp", "context"), "tensor"),
        P("tensor"),
        P("tensor"),
        P("tensor"),
        P(None, "tensor"),
        P("tensor"),
        P("tensor"),
        P("tensor", None),
        P(("dp", "context"), "tensor"),
        P(),
        P("context", "tensor"),
        P("context", "tensor"),
        P("context", "tensor"),
        P(("dp", "context")),
        P(("dp", "context"), None),
    )
    out_specs = (P(("dp", "context"), "tensor"), P(("dp", "context"), "tensor"))
    return jax.shard_map(
        per_device, mesh=mesh, in_specs=in_specs, out_specs=out_specs, check_vma=False
    )
```

time: 806 us -> 132 us (0.16)
  waiting for transfers between devices: 576 us -> 0 us
  Pallas kernels: 0 us -> 127 us
  blocking collectives: 108 us -> 0 us
  matrix products: 53.3 us -> 0 us
  other arithmetic: 35.6 us -> 0 us
  between operations: 18.9 us -> 0.65 us
    all_gather x7 -> x0, waiting for transfers between devices: 492 us -> none  [the longest x1 95.6 us: carried_in(): gathered = jax.tree.map(lambda a: lax.all_gather(a, axis), part)]
    pallas_call x0 -> x1, Pallas kernels: none -> 127 us  [layer(): pl.pallas_call(kernel, out_shape=(jax.ShapeDtypeStruct((2, half, share),...]
    reduce_scatter x1 -> x0, waiting for transfers between devices: 82.3 us -> none  [per_device(): lax.psum_scatter(partial_value, 'tensor', scatter_dimension=1, tiled=True)]
    all_gather x2 -> x0, blocking collectives: 81.4 us -> none  [the longest x1 44.5 us: per_device(): all_docs = lax.all_gather(doc_ids, 'context', axis=0, tiled=True)]
    dot_general x10 -> x0, matrix products: 53.3 us -> none  [the longest x1 15.2 us: update(): jnp.einsum('kgqr,rkd->kgqd', probs.astype(jnp.bfloat16), value_piece.resh...]
    all_to_all x1 -> x0, blocking collectives: 17.6 us -> none  [per_device(): lax.all_to_all(outgoing, 'context', split_axis=0, concat_axis=0, tiled=True)]
    reduce_sum x4 -> x0, other arithmetic: 16.5 us -> none  [the longest x1 14.5 us: update(): denom = jnp.sum(probs, axis=-1)]
    psum x1 -> x0, blocking collectives: 8.58 us -> none  [per_device(): squares = lax.psum(jnp.sum(stream_float * stream_float, axis=-1), 'tensor')]
  transfers between devices with their start and end apart: 9 -> 0, of which waited for: 8 -> 0; matrix products, arithmetic and copies ran while one was open for 4% -> 0% of each run, Pallas kernels for 0% -> 0%
where the time goes in v4:
time: 132 us; the launch traced here: 131 us
  Pallas kernels  127 us (96%)
  local copies, waits for them, and re-layouts  3.54 us (3%)
    pallas_call x1, Pallas kernels, layer(): pl.pallas_call(kernel, out_shape=(jax.ShapeDtypeStruct((2, half, share),...  127 us
    unnamed x2, local copies, waits for them, and re-layouts  3.54 us

profile of v4, /device:TPU:32, one launch (start us, length us, event | category | flops | bytes accessed | tf_op | source)
XLA Modules:
  0.0 130.7 jit_solution(2037542459306463385)
XLA Ops:
  0.6 126.6 %layer.1 = (bf16[2,128,1024]{2,1,0:T(8,128)(2,1)}, bf16[32,8,512]{2,1,0:T(8,128)(2,1)}) custom-call(bf16[256,1280]{1,0:T(8,128)(2,1)} %refs_0_.1, bf16[256,1024]{1,0:T(8,128)(2,1)} %refs_1_.1, f32[16,256]{1,0:T(8,128)} %bitcast.12, s32[2,128]{1,0:T(2,128)} %bitcast.16, f32[4,1280]{1,0:T(4,128)} %refs_4_.1, f32[10,128]{1,0:T(8,128)} %bitcast.14, ...), custom_call_target="tpu_custom_call" | custom-call | tf_op jit(solution)/shard_map/layer/pallas_call | solution.py:973
  127.2 1.9 %copy.21 = bf16[256,1024]{1,0:T(8,128)(2,1)} copy(bf16[256,1024]{1,0:T(8,128)(2,1)} %bitcast.10) | data formatting | bytes 1048576
  129.1 1.7 %copy.22 = bf16[256,512]{1,0:T(8,128)(2,1)} copy(bf16[256,512]{1,0:T(8,128)(2,1)} %bitcast.11) | data formatting | bytes 524288

commit v5 on v4

--- a/solution.py
+++ b/solution.py
@@ -50,6 +50,17 @@
 
 def around(first, count, step, carry=None):
     lax.fori_loop(first, count, lambda number, none: (step(number), none)[1], 0)
+
+
+def cross_copy(r, row, col, core, place, direction, source=None):
+    target = lax.rem(row + (1 if direction == 0 else N_Y - 1), N_Y)
+    return remote(
+        r.shards.at[place] if source is None else source,
+        r.gathered.at[row * N_Z + place, core],
+        r.cross_send.at[direction, place],
+        r.cross_recv.at[direction, place],
+        context_peer(target * N_Z + col),
+    )
 
 
 def mix_phase(r, me, core):
@@ -189,6 +200,10 @@
         place = lax.rem(col + distance, N_Z)
         return shard_copy(place, distance, r.down_send, r.down_recv, below)
 
+    def spread_shard(place):
+        cross_copy(r, row, col, core, place, 0).start()
+        cross_copy(r, row, col, core, place, 1).start()
+
     halo_docs.wait_recv()
     r.docs_ext[:pad] = jnp.where(me > 0, r.docs_ext[:pad], -1.0)
     halo_rows.wait_recv()
@@ -260,6 +275,8 @@
     r.recv[me] = r.pieces[me]
     r.side_all[me] = r.side[me]
     r.shards[col] = r.shard[...]
+    cross_copy(r, row, col, core, col, 0, r.shard).start()
+    cross_copy(r, row, col, core, col, 1, r.shard).start()
 
     mixing = lax.dot_general(out_c, in_b, nt, preferred_element_type=jnp.float32)
     docs_wide = jnp.concatenate([docs_col, docs_col], axis=1)
@@ -309,6 +326,8 @@
         if distance < 3:
             shard_down(distance - 1).wait_recv()
             shard_down(distance).start()
+            spread_shard(lax.rem(col + distance, N_Z))
+        spread_shard(lax.rem(col + N_Z - distance, N_Z))
 
     shard_turn(1)
     r.load_gate.wait()
@@ -358,7 +377,9 @@
 
     def shards_arrive():
         shard_down(2).wait_recv()
+        spread_shard(lax.rem(col + 3, N_Z))
         shard_up(3).wait_recv()
+        spread_shard(lax.rem(col + 4, N_Z))
         around(1, N_CTX, docs_arrive)
 
     return finish, shards_arrive
@@ -403,7 +424,7 @@
     def row_copy(owner_row, begin, count, number, target_row):
         part = r.gathered.at[pl.ds(owner_row * N_Z + begin, count), core]
         return remote(
-            r.shards if number < 2 else part,
+            part,
             part,
             r.y_send.at[number],
             r.y_recv.at[number],
@@ -430,8 +451,6 @@
     rs[3].start()
 
     shards_arrive()
-    row_copy(row, 0, N_Z, 0, up).start()
-    row_copy(row, 0, N_Z, 1, down).start()
     core_copy(row, 0, core, r.shards).start()
 
     rs[0].wait_recv()
@@ -444,6 +463,12 @@
     r.hold_a[...] = product[:half]
     r.hold_b[...] = product[half:]
     r.gathered[pl.ds(row * N_Z, N_Z), core] = r.shards[...]
+    around(0, N_Z, lambda place: cross_copy(r, down, col, core, place, 0).wait_recv())
+    row_copy(down, 0, quarter, 2, up).start()
+    core_copy(down, 1).start()
+    around(0, N_Z, lambda place: cross_copy(r, up, col, core, place, 1).wait_recv())
+    row_copy(up, quarter, quarter, 3, down).start()
+    core_copy(up, 2).start()
 
     def full_copy(owner, part, number, target):
         return remote(
@@ -505,13 +530,6 @@
     full_copy(right, 1, 3, left).wait_recv()
     full_copy(right, 1, 5, left).start()
 
-    row_copy(down, 0, N_Z, 0, up).wait_recv()
-    row_copy(down, 0, quarter, 2, up).start()
-    core_copy(down, 1).start()
-    row_copy(up, 0, N_Z, 1, down).wait_recv()
-    row_copy(up, quarter, quarter, 3, down).start()
-    core_copy(up, 2).start()
-
     full_copy(left, 1, 1, right).wait_recv()
     full_copy(right, 0, 2, left).wait_recv()
 
@@ -535,7 +553,6 @@
             stream = r.full[owner, part].astype(jnp.float32)
             squares = squares + jnp.sum(stream * stream, axis=1, keepdims=True)
         scale = lax.rsqrt(squares / (N_T * width) + epsilon)
-        total = jnp.zeros((half, out_width), jnp.float32)
         for owner in range(N_T):
             stream = r.full[owner, part].astype(jnp.float32)
             gain = jnp.concatenate(
@@ -545,27 +562,39 @@
                 ],
                 axis=1,
             )
-            block = (stream * scale * gain).astype(jnp.bfloat16)
-            piece = r.gathered[owner * rows_each : (owner + 1) * rows_each].reshape(
-                depth, out_width
+            r.block[part, owner] = (stream * scale * gain).astype(jnp.bfloat16)
+    pair_begin = out_width - 2 * HEAD_DIMENSION
+
+    def product_of(part, begin, count):
+        total = jnp.zeros((half, count), jnp.float32)
+        for owner in range(N_T):
+            piece = r.gathered[
+                owner * rows_each : (owner + 1) * rows_each, :, :, begin : begin + count
+            ].reshape(depth, count)
+            total = total + jnp.dot(
+                r.block[part, owner], piece, preferred_element_type=jnp.float32
             )
-            total = total + jnp.dot(block, piece, preferred_element_type=jnp.float32)
+        return total
+
+    def turn(value, rows):
+        return value * r.cosine[rows] + pltpu.roll(value, HEAD_DIMENSION // 2, 1) * r.sine[rows]
+
+    for part in range(2):
         rows = slice(part * half, (part + 1) * half)
-        count = out_width // HEAD_DIMENSION
-        for head in range(count):
-            lanes = slice(head * HEAD_DIMENSION, (head + 1) * HEAD_DIMENSION)
-            value = total[:, lanes]
-            if head < count - 1:
-                value = (
-                    value * r.cosine[rows] + pltpu.roll(value, HEAD_DIMENSION // 2, 1) * r.sine[rows]
+        total = product_of(part, pair_begin, 2 * HEAD_DIMENSION)
+        r.window[0, part] = turn(total[:, :HEAD_DIMENSION], rows).astype(jnp.bfloat16)
+        r.window[0, 2 + part] = total[:, HEAD_DIMENSION:].T.astype(jnp.bfloat16)
+
+    def make_queries():
+        for part in range(2):
+            rows = slice(part * half, (part + 1) * half)
+            total = product_of(part, 0, pair_begin)
+            for head in range(pair_begin // HEAD_DIMENSION):
+                value = turn(
+                    total[:, head * HEAD_DIMENSION : (head + 1) * HEAD_DIMENSION], rows
                 )
-            if head < count - 2:
                 begin = head * tokens + part * half
                 r.queries[:, begin : begin + half] = value.T.astype(jnp.bfloat16)
-            elif head < count - 1:
-                r.window[0, part] = value.astype(jnp.bfloat16)
-            else:
-                r.window[0, 2 + part] = value.T.astype(jnp.bfloat16)
 
     def finish():
         for copy in rs:
@@ -576,18 +605,22 @@
         full_copy(me, 0, 2, left).wait_send()
         full_copy(left, 0, 4, right).wait_send()
         full_copy(right, 1, 5, left).wait_send()
-        row_copy(row, 0, N_Z, 0, up).wait_send()
-        row_copy(row, 0, N_Z, 1, down).wait_send()
+
+        def crossed(place):
+            cross_copy(r, row, col, core, place, 0).wait_send()
+            cross_copy(r, row, col, core, place, 1).wait_send()
+
+        around(0, N_Z, crossed)
         row_copy(down, 0, quarter, 2, up).wait_send()
         row_copy(up, quarter, quarter, 3, down).wait_send()
         for number, owner in enumerate((row, down, up, far)):
             core_copy(owner, number).wait_send()
         hidden_out.wait()
 
-    return finish
-
-
-def attend_phase(r, me):
+    return finish, make_queries
+
+
+def attend_phase(r, me, make_queries):
     number = r.queries.shape[1]
     tokens = 2 * r.window.shape[2]
     group = number // tokens
@@ -675,6 +708,7 @@
         def _():
             send_up(0, part).start()
 
+    make_queries()
     attend_first()
 
     visits = (8, 1, 7, 16, 9, 2, 6, 15, 10, 3, 14, 5, 17, 11, 13, 4, 12)
@@ -686,8 +720,6 @@
         for number_here, value in enumerate(visits):
             slot = jnp.where(step == number_here, value, slot)
         upward = (slot >= up_base) & (slot <= up_base + 3)
-        downward = ((slot >= 6) & (slot <= 8)) | ((slot >= 13) & (slot <= 16))
-        crossing = (slot <= 3) | (slot == 8) | (slot == 9)
         for part in range(4):
             remote(
                 window.at[slot, part],
@@ -696,6 +728,10 @@
                 r.win_recv_sem.at[slot, part],
                 context_peer(forward),
             ).wait_recv()
+
+            last_down, last_cross = (13, 3) if part < 2 else (14, 4)
+            downward = ((slot >= 6) & (slot <= 8)) | ((slot >= last_down) & (slot <= 16))
+            crossing = (slot <= last_cross) | (slot == 8) | (slot == 9)
 
             @pl.when(crossing)
             def _():
@@ -756,9 +792,9 @@
     for part in range(4):
         for slot in range(4):
             send_up(slot + up_base, part).wait_send()
-        for slot in goes_down:
+        for slot in goes_down if part < 2 else goes_down[:3] + goes_down[4:]:
             send_down(slot, part).wait_send()
-        for slot in (0,) + goes_across:
+        for slot in (0,) + goes_across + (() if part < 2 else (4,)):
             send_across(slot, part).wait_send()
 
     def finish():
@@ -870,10 +906,13 @@
         rs_recv=DMA((6,)),
         ag_send=DMA((6,)),
         ag_recv=DMA((6,)),
+        cross_send=DMA((2, N_Z)),
+        cross_recv=DMA((2, N_Z)),
         y_send=DMA((4,)),
         y_recv=DMA((4,)),
         core_send=DMA((4,)),
         core_recv=DMA((4,)),
+        block=VMEM((2, N_T, half, share), bf),
         queries=VMEM((HEAD_DIMENSION, group * rows), bf),
         window=VMEM((WINDOW, 4, half, HEAD_DIMENSION), bf),
         outgoing=VMEM(out_rows, bf),
@@ -962,9 +1001,9 @@
             r.load_tiles.append(copy)
 
         finish_mix, shards_arrive = mix_phase(r, me, core)
-        finish_project = project_phase(r, me, core, shards_arrive)
+        finish_project, make_queries = project_phase(r, me, core, shards_arrive)
         load_owners.wait()
-        finish_attend = attend_phase(r, me)
+        finish_attend = attend_phase(r, me, make_queries)
         finish_mix()
         finish_project()
         finish_attend()

time: 132 us -> 129 us (0.977)
  Pallas kernels: 127 us -> 125 us
    pallas_call x1, Pallas kernels: 127 us -> 125 us  [layer(): pl.pallas_call(kernel, out_shape=(jax.ShapeDtypeStruct((2, half, share),...]
where the time goes in v5:
time: 129 us
  Pallas kernels  125 us (97%)
  local copies, waits for them, and re-layouts  3.54 us (3%)
    pallas_call x1, Pallas kernels, layer(): pl.pallas_call(kernel, out_shape=(jax.ShapeDtypeStruct((2, half, share),...  125 us
    unnamed x2, local copies, waits for them, and re-layouts  3.54 us

profile of v5, /device:TPU:32, one launch (start us, length us, event | category | flops | bytes accessed | tf_op | source)
XLA Modules:
  0.0 129.0 jit_solution(16177760162405239250)
XLA Ops:
  0.6 124.8 %layer.1 = (bf16[2,128,1024]{2,1,0:T(8,128)(2,1)}, bf16[32,8,512]{2,1,0:T(8,128)(2,1)}) custom-call(bf16[256,1280]{1,0:T(8,128)(2,1)} %refs_0_.1, bf16[256,1024]{1,0:T(8,128)(2,1)} %refs_1_.1, f32[16,256]{1,0:T(8,128)} %bitcast.12, s32[2,128]{1,0:T(2,128)} %bitcast.16, f32[4,1280]{1,0:T(4,128)} %refs_4_.1, f32[10,128]{1,0:T(8,128)} %bitcast.14, ...), custom_call_target="tpu_custom_call" | custom-call | tf_op jit(solution)/shard_map/layer/pallas_call | solution.py:1012
  125.5 1.9 %copy.21 = bf16[256,1024]{1,0:T(8,128)(2,1)} copy(bf16[256,1024]{1,0:T(8,128)(2,1)} %bitcast.10) | data formatting | bytes 1048576
  127.4 1.7 %copy.22 = bf16[256,512]{1,0:T(8,128)(2,1)} copy(bf16[256,512]{1,0:T(8,128)(2,1)} %bitcast.11) | data formatting | bytes 524288
